TPU v7x, 128 devices: a whole 4x4x4 slice. The times are simulated.
128 devices in a mesh: row: 16 (over y, z), col: 8 (over x, core).
Axes of the slice: x: 4, y: 4, z: 4, core: 2. Of those that a mesh axis runs over, the one named last changes fastest.
Arguments:
- glob_derivs: bfloat16 [128, 16, 256, 128], P(('row', 'col')), may hold values from -0.09375 to 0.09375
- local_derivs: float32 [128, 16, 4, 256], P(('row', 'col')), may hold values from -6 to 6
- weights: float32 [128, 16, 256], P(('row', 'col')), may hold values from 0.25 to 4
- residuals: float32 [128, 16, 256], P(('row', 'col')), may hold values from -6 to 6
- track_ids: int32 [128, 16, 256], P(('row', 'col')), may hold values from 0 to 255
- module_blocks: int32 [128, 16], replicated, may hold values from 0 to 7
- weak_modes: float32 [16384, 64], P('col'), may hold values from -6 to 6
Outputs:
- schur: float32 [16384, 16384], P('row', 'col')
- layer_blocks: float32 [16384, 1024], P('row', 'col')
- rhs: float32 [16384], P('row')
- weak_product: float32 [16384, 64], P(('row', 'col'))
All inputs are finite; a program needn't handle non-finite values.
Results may differ from a plain program's by a relative error of at most 0.0094.
Values sent between devices are 32-bit elements; how exact they have to be, the bound alone decides.
A program may use at most 128 MiB of HBM per device.

v0:
```python
import jax
import jax.numpy as jnp
from jax import lax
from jax.sharding import PartitionSpec as P

BW = 128
GB = 8
LOC = 4
TRK = 256


def broadcast(block, axis, source):
    block = jnp.where(lax.axis_index(axis) == source, block, jnp.zeros_like(block))
    return lax.psum(block, axis)


def invert(matrix):
    count = matrix.shape[0]
    rows = [matrix[i] for i in range(count)]
    inverse = [jnp.zeros_like(matrix[0]).at[i].set(1.0) for i in range(count)]
    for pivot_row in range(count):
        pivot = rows[pivot_row][pivot_row]
        scaled = rows[pivot_row] / pivot
        scaled_inv = inverse[pivot_row] / pivot
        for other in range(count):
            if other != pivot_row:
                factor = rows[other][pivot_row]
                rows[other] = rows[other] - factor * scaled
                inverse[other] = inverse[other] - factor * scaled_inv
        rows[pivot_row] = scaled
        inverse[pivot_row] = scaled_inv
    return jnp.stack(inverse)


def bundle_terms(glob, local, weight, resid, tracks):
    layers = glob.shape[0]
    f32 = jnp.float32
    onehot = (tracks[:, :, None] == jnp.arange(TRK)[None, None, :]).astype(f32)
    weighted = weight[:, None, :] * local
    weighted_low = weighted.astype(jnp.bfloat16)
    hot_low = onehot.astype(jnp.bfloat16)
    h_parts = []
    for lidx in range(LOC):
        spread_one = hot_low * weighted_low[:, lidx, :, None]
        h_parts.append(jnp.einsum("spi,spt->sit", glob, spread_one, preferred_element_type=f32))
    h_mat = jnp.stack(h_parts, axis=3).reshape(layers, BW, TRK * LOC).astype(jnp.bfloat16)
    prods = weighted[:, :, None, :] * local[:, None, :, :]
    normal = jnp.einsum("sijm,smt->ijt", prods, onehot, precision=lax.Precision.HIGHEST)
    normal = normal + jnp.eye(LOC, dtype=f32)[:, :, None]
    qvec = jnp.einsum(
        "sjm,smt->jt", weighted * resid[:, None, :], onehot, precision=lax.Precision.HIGHEST
    )
    kinv = invert(normal)
    h_wide = h_mat.astype(f32).reshape(layers, BW, TRK, LOC)
    x_wide = jnp.zeros_like(h_wide)
    for lidx in range(LOC):
        x_wide = x_wide + h_wide[..., lidx : lidx + 1] * jnp.transpose(kinv[lidx])[None, None]
    x_mat = x_wide.reshape(layers, BW, TRK * LOC).astype(jnp.bfloat16)
    wglob = (weight[:, :, None] * glob.astype(f32)).astype(jnp.bfloat16)
    diag_tiles = jnp.einsum("spi,spj->sij", wglob, glob, preferred_element_type=f32)
    wres = (weight * resid).astype(jnp.bfloat16)
    qflat = jnp.transpose(qvec).reshape(TRK * LOC).astype(jnp.bfloat16)
    vec = jnp.einsum("sp,spi->si", wres, glob, preferred_element_type=f32) - jnp.einsum(
        "sik,k->si", x_mat, qflat, preferred_element_type=f32
    )
    gram = jnp.einsum("rip,ljp->rlij", x_mat, h_mat, preferred_element_type=f32)
    tiles = jnp.eye(layers, dtype=f32)[:, :, None, None] * diag_tiles[:, None, :, :] - gram
    return (tiles, vec)


def body(glob_derivs, local_derivs, weights, residuals, track_ids, module_blocks, weak_modes):
    tiles, vec = bundle_terms(
        glob_derivs[0], local_derivs[0], weights[0], residuals[0], track_ids[0]
    )
    layers = tiles.shape[0]
    n_col = lax.axis_size("col")
    groups = layers // n_col
    row_index = lax.axis_index("row")
    col_index = lax.axis_index("col")
    row_blocks = lax.dynamic_slice_in_dim(module_blocks, row_index, 1, 1)[:, 0]
    row_hot = (row_blocks[:, None] == jnp.arange(GB)[None, :]).astype(jnp.float32)
    vec_out = jnp.repeat(vec, n_col, axis=0)
    outgoing = tiles.reshape(layers * n_col, groups, BW, BW)
    incoming = (
        lax.all_to_all(outgoing, ("row", "col"), split_axis=0, concat_axis=0, tiled=True),
        lax.all_to_all(vec_out, ("row", "col"), split_axis=0, concat_axis=0, tiled=True),
    )
    in_tiles = incoming[0]
    in_vec = incoming[1]
    rhs = jnp.einsum("bk,bi->ki", row_hot, in_vec, precision=lax.Precision.HIGHEST).reshape(GB * BW)
    col_blocks = lax.dynamic_slice_in_dim(module_blocks, col_index * groups, groups, 1)
    col_hot = (col_blocks[:, :, None] == jnp.arange(GB)[None, None, :]).astype(jnp.float32)
    pairs = row_hot[:, None, :, None] * col_hot[:, :, None, :]
    placed = jnp.einsum("bqkl,bqij->kiqlj", pairs, in_tiles, precision=lax.Precision.HIGHEST)
    product = jnp.dot(
        placed.reshape(GB * BW, groups * GB * BW),
        weak_modes,
        precision=lax.Precision.HIGHEST,
        preferred_element_type=jnp.float32,
    )
    weak_product = lax.psum_scatter(product, "col", scatter_dimension=0, tiled=True)
    own_slot = jnp.clip(row_index - col_index * groups, 0, groups - 1)
    candidate = lax.dynamic_index_in_dim(placed, own_slot, 2, False).reshape(GB * BW, GB * BW)
    square = broadcast(candidate, "col", row_index // groups)
    width = GB * BW // n_col
    layer_blocks = lax.dynamic_slice_in_dim(square, col_index * width, width, 1)
    col_layers = col_index * groups + jnp.arange(groups)
    keep_mask = (col_layers != row_index).astype(jnp.float32)
    schur = (placed * keep_mask[None, None, :, None, None]).reshape(GB * BW, groups * GB * BW)
    return (schur, layer_blocks, rhs, weak_product)


def solution(mesh):
    placed = (
        P(("row", "col"), None, None, None),
        P(("row", "col"), None, None, None),
        P(("row", "col"), None, None),
        P(("row", "col"), None, None),
        P(("row", "col"), None, None),
        P(),
        P("col", None),
    )
    return jax.shard_map(
        body,
        mesh=mesh,
        in_specs=placed,
        out_specs=(P("row", "col"), P("row", "col"), P("row"), P(("row", "col"), None)),
        check_vma=False,
    )
```

profile of v0, /device:TPU:17, one launch (start us, length us, event | category | flops | bytes accessed | tf_op | source)
XLA Modules:
  0.0 473.7 jit_solution(15043064537932152104)
XLA Ops:
  17.2 2.9 fusion.48
  20.1 2.9 fusion.45
  23.1 2.9 fusion.42
  28.5 3.4 slice_bitcast_fusion.3
  34.7 3.0 copy.52
  37.7 3.0 copy.51
  40.7 2.9 copy.50
  43.7 5.0 %add_convert_fusion = bf16[16,128,256,4]{2,1,3,0:T(8,128)(2,1)S(1)} fusion(f32[256,4]{0,1:T(4,128)S(1)} %get-tuple-element.55, f32[16,128,256]{2,1,0:T(8,128)} %copy.52, f32[256,4]{0,1:T(4,128)S(1)} %get-tuple-element.78, f32[16,128,256]{2,1,0:T(8,128)} %copy.51, f32[256,4]{0,1:T(4,128)S(1)} %get-tuple-element.77, f32[16,128,256]{2,1,0:T(8,128)} %copy.50, ...), kind=kLoop, calls=%fused_computation.3 | loop fusion | flops 16777216 | bytes 12599296 | tf_op jit(solution)/shard_map/convert_element_type | solution.py:58
  50.8 12.9 %bitcast_subtract_fusion = f32[16,16,128,128]{2,3,0,1:T(8,128)} fusion(f32[16,128,128]{1,2,0:T(8,128)S(1)} %fusion.26, f32[16,16]{0,1:T(8,128)S(1)} %fusion.84, bf16[16,128,256,4]{2,1,3,0:T(8,128)(2,1)S(1)} %add_convert_fusion, bf16[16,128,256,4,1]{1,2,0,3,4:T(8,128)(2,1)S(1)} %copy-done.4), kind=kOutput, calls=%fused_computation | convolution fusion | flops 8598323200 | bytes 26215424 | tf_op jit(solution)/shard_map/rip,ljp->rlij/dot_general | solution.py:66
  63.8 17.6 %copy.54 = f32[16,16,128,128]{3,2,1,0:T(8,128)} copy(f32[16,16,128,128]{2,3,0,1:T(8,128)} %bitcast_subtract_fusion) | data formatting | bytes 33554432 | tf_op jit(solution)/shard_map/sub | solution.py:67
  81.4 11.1 %all-to-all-start = ((f32[128,2,128,128]{3,2,1,0:T(8,128)}), f32[128,2,128,128]{3,2,1,0:T(8,128)}, u32[]{:S(2)}, u32[]{:S(2)}) async-start(f32[128,2,128,128]{3,2,1,0:T(8,128)} %bitcast.161), calls=%async_computation | async-start | bytes 33554432 | tf_op jit(solution)/shard_map/all_to_all | solution.py:85
  94.0 222.6 %all-to-all-done = f32[128,2,128,128]{3,2,1,0:T(8,128)} async-done(((f32[128,2,128,128]{3,2,1,0:T(8,128)}), f32[128,2,128,128]{3,2,1,0:T(8,128)}, u32[]{:S(2)}, u32[]{:S(2)}) %all-to-all-start) | async-done | bytes 16777248 | tf_op jit(solution)/shard_map/all_to_all | solution.py:85
  316.6 26.2 %broadcast_multiply_fusion = (f32[8,128,2,8,128]{4,3,0,1,2:T(8,128)}, f32[2,128,128,8,8]{2,4,3,1,0:T(8,128)S(1)}) fusion(f32[2]{0:T(128)S(1)} %compare_convert_fusion, f32[128,2,8]{0,2,1:T(8,128)S(1)} %fusion.85, f32[128,8]{0,1:T(8,128)S(1)} %fusion.92, f32[128,2,128,128,1]{3,2,1,0,4:T(8,128)} %bitcast.49), kind=kOutput, calls=%fused_computation.9 | convolution fusion | flops 3223339008 | bytes 33566728 | tf_op jit(solution)/shard_map/bqkl,bqij->kiqlj/dot_general | solution.py:94
  346.4 3.0 copy.97
  350.9 3.4 fusion.90
  354.3 7.4 %copy.59 = f32[8,128,2,8,128]{4,3,2,1,0:T(8,128)} copy(f32[8,128,2,8,128]{4,3,0,1,2:T(8,128)} %bitcast.162) | data formatting | bytes 16777216 | tf_op jit(solution)/shard_map/bqkl,bqij->kiqlj/transpose | solution.py:94
  361.7 9.3 %reshape.223 = f32[1024,2048]{1,0:T(8,128)} reshape(f32[8,128,2,8,128]{4,3,2,1,0:T(8,128)} %copy.59) | data formatting | bytes 16777216 | tf_op jit(solution)/shard_map/reshape | solution.py:96
  371.0 11.4 %fusion.98 = f32[1024,64]{0,1:T(8,128)} fusion(f32[1024,2048]{1,0:T(8,128)} %reshape.223, f32[2048,64]{0,1:T(8,128)S(1)} %copy-done), kind=kOutput, calls=%fused_computation.121 | convolution fusion | flops 1610612736 | bytes 9175040 | tf_op jit(solution)/shard_map/dot_general | solution.py:95
  383.4 21.8 %all-to-all-start.1 = ((f32[128,1,128]{2,1,0:T(1,128)}), f32[128,1,128]{2,1,0:T(1,128)S(1)}, u32[]{:S(2)}, u32[]{:S(2)}) async-start(f32[128,1,128]{2,1,0:T(1,128)} %bitcast.63), calls=%async_computation.1 | async-start | bytes 131072 | tf_op jit(solution)/shard_map/all_to_all | solution.py:86
  405.2 7.7 %all-to-all-done.1 = f32[128,1,128]{2,1,0:T(1,128)S(1)} async-done(((f32[128,1,128]{2,1,0:T(1,128)}), f32[128,1,128]{2,1,0:T(1,128)S(1)}, u32[]{:S(2)}, u32[]{:S(2)}) %all-to-all-start.1) | async-done | bytes 65568 | tf_op jit(solution)/shard_map/all_to_all | solution.py:86
  413.7 7.6 %copy.56 = f32[8,128,2,8,128]{4,3,2,1,0:T(8,128)} copy(f32[8,128,2,8,128]{4,3,0,1,2:T(8,128)} %get-tuple-element.85) | data formatting | bytes 16777216 | tf_op jit(solution)/shard_map/mul | solution.py:109
  421.2 9.3 %reshape.221 = f32[1024,2048]{1,0:T(8,128)} reshape(f32[8,128,2,8,128]{4,3,2,1,0:T(8,128)} %copy.56) | data formatting | bytes 16777216 | tf_op jit(solution)/shard_map/reshape | solution.py:109
  430.5 3.1 all-reduce.2.cloned.1.call-done
  435.5 31.4 %reduce-scatter.2.cloned.1.call-done = f32[128,64]{0,1:T(8,128)} async-done(((f32[1024,64]{0,1:T(8,128)}), f32[128,64]{0,1:T(8,128)}) %reduce-scatter.2.cloned.1.call-update) | async-done | bytes 32784 | tf_op jit(solution)/shard_map/reduce_scatter | solution.py:101
  (71 shorter events, 27.3 us)
Async XLA Ops:
  7.2 363.9 %copy-start = (f32[2048,64]{0,1:T(8,128)S(1)}, f32[2048,64]{0,1:T(8,128)}, u32[]{:S(2)}) copy-start(f32[2048,64]{0,1:T(8,128)} %param.21) | copy-start | bytes 1572868
  7.2 7.1 %copy-start.11 = (s32[1,16,256]{2,1,0:T(8,128)S(1)}, s32[1,16,256]{2,1,0:T(8,128)}, u32[]{:S(2)}) copy-start(s32[1,16,256]{2,1,0:T(8,128)} %param.19) | copy-start | bytes 49156
  7.2 7.1 %copy-start.3 = (bf16[1,16,256,128]{3,2,1,0:T(8,128)(2,1)S(1)}, bf16[1,16,256,128]{3,2,1,0:T(8,128)(2,1)}, u32[]{:S(2)}) copy-start(bf16[1,16,256,128]{3,2,1,0:T(8,128)(2,1)} %param.15) | copy-start | bytes 3145732
  37.7 5.9 %copy-start.7 = (f32[256,4]{0,1:T(4,128)S(1)}, f32[256,4]{0,1:T(4,128)}, u32[]{:S(2)}) copy-start(f32[256,4]{0,1:T(4,128)} %constant.162.clone.1) | copy-start | bytes 12292
  37.7 5.9 %copy-start.8 = (f32[256,4]{0,1:T(4,128)S(1)}, f32[256,4]{0,1:T(4,128)}, u32[]{:S(2)}) copy-start(f32[256,4]{0,1:T(4,128)} %constant.161.clone.1) | copy-start | bytes 12292
  37.7 6.0 %copy-start.9 = (f32[256,4]{0,1:T(4,128)S(1)}, f32[256,4]{0,1:T(4,128)}, u32[]{:S(2)}) copy-start(f32[256,4]{0,1:T(4,128)} %constant.164.clone.1) | copy-start | bytes 12292
  37.7 6.0 %copy-start.10 = (f32[256,4]{0,1:T(4,128)S(1)}, f32[256,4]{0,1:T(4,128)}, u32[]{:S(2)}) copy-start(f32[256,4]{0,1:T(4,128)} %constant.163.clone.1) | copy-start | bytes 12292
  43.7 7.1 %copy-start.4 = (bf16[16,128,256,4,1]{1,2,0,3,4:T(8,128)(2,1)S(1)}, bf16[16,128,256,4,1]{1,2,0,3,4:T(8,128)(2,1)}, u32[]{:S(2)}) copy-start(bf16[16,128,256,4,1]{1,2,0,3,4:T(8,128)(2,1)} %get-tuple-element.65) | copy-start | bytes 12582916
  48.8 2.1 copy-start.2
  81.4 235.2 %all-to-all-start = ((f32[128,2,128,128]{3,2,1,0:T(8,128)}), f32[128,2,128,128]{3,2,1,0:T(8,128)}, u32[]{:S(2)}, u32[]{:S(2)}) async-start(f32[128,2,128,128]{3,2,1,0:T(8,128)} %bitcast.161), calls=%async_computation | async-start | bytes 33554432 | tf_op jit(solution)/shard_map/all_to_all | solution.py:85
  92.5 341.1 %all-reduce.2.cloned.1.call-start = ((), (), s32[]{:S(2)}) async-start(), calls=%async_computation.3 | async-start | bytes 8388608 | tf_op jit(solution)/shard_map/psum | solution.py:14
  342.8 3.3 copy-start.1
  349.4 1.5 copy-start.5
  349.4 1.5 copy-start.6
  349.4 117.4 %reduce-scatter.2.cloned.1.call-start = ((), (), s32[]{:S(2)}) async-start(), calls=%async_computation.4 | async-start | bytes 294912 | tf_op jit(solution)/shard_map/reduce_scatter | solution.py:101
  383.4 29.6 %all-to-all-start.1 = ((f32[128,1,128]{2,1,0:T(1,128)}), f32[128,1,128]{2,1,0:T(1,128)S(1)}, u32[]{:S(2)}, u32[]{:S(2)}) async-start(f32[128,1,128]{2,1,0:T(1,128)} %bitcast.63), calls=%async_computation.1 | async-start | bytes 131072 | tf_op jit(solution)/shard_map/all_to_all | solution.py:86
Sparse Core Ops, SparseCore 0:
  349.5 84.0 all-reduce.1
  436.5 30.2 reduce-scatter.1
where the time goes:
time: 478 us; the launch traced here: 474 us
  waiting for transfers between devices  265 us (55%)
  local copies, waits for them, and re-layouts  79.2 us (17%)
  matrix products  72.9 us (15%)
  starting transfers between devices  33 us (7%)
  between operations  14.4 us (3%)
  other arithmetic  9.31 us (2%)
    all_to_all x1, waiting for transfers between devices, body(): lax.all_to_all(outgoing, ('row', 'col'), split_axis=0, concat_axis=0, til...  223 us
    reduce_scatter x1, waiting for transfers between devices, body(): lax.psum_scatter(product, 'col', scatter_dimension=0, tiled=True)  31.4 us
    dot_general x1, matrix products, body(): jnp.einsum('bqkl,bqij->kiqlj', pairs, in_tiles, precision=lax.Precision.H...  26.2 us
    all_to_all x1, starting transfers between devices, body(): lax.all_to_all(vec_out, ('row', 'col'), split_axis=0, concat_axis=0, tile...  21.8 us
    sub x1, local copies, waits for them, and re-layouts, bundle_terms(): jnp.eye(layers, dtype=f32)[:, :, None, None] * diag_tiles[:, None, :, :]  17.6 us
    mul x5, local copies, waits for them, and re-layouts, bundle_terms(): h_wide[..., lidx:lidx + 1] * jnp.transpose(kinv[lidx])[None, None]  15.1 us
    dot_general x1, matrix products, bundle_terms(): gram = jnp.einsum('rip,ljp->rlij', x_mat, h_mat, preferred_element_type=f32)  12.9 us
    dot_general x4, matrix products, bundle_terms(): jnp.einsum('spi,spt->sit', glob, spread_one, preferred_element_type=f32)  11.7 us
  transfers between devices with their start and end apart: 4, of which 4 were waited for; matrix products, arithmetic and copies ran while one was open for 12% of the time, Pallas kernels for 0%

commit v1 on v0

v1 whole, which is shorter than its diff:
```python
import functools

import jax
import jax.numpy as jnp
from jax import lax
from jax.experimental import pallas as pl
from jax.experimental.pallas import tpu as pltpu
from jax.sharding import PartitionSpec as P

BW = 128
GB = 8
LOC = 4
TRK = 256
LAYERS = 16
PER = 256
ROWS = 88
SIZE = {"y": 4, "z": 4, "X": 8}
ORDERS = (("y", "z", "X"), ("z", "X", "y"), ("X", "y", "z"))
RING = (1, 3, 2)
WIDE = (2, 3, 6, 7, 1, 4, 5)
MESH = pl.DeviceIdType.MESH
f32 = jnp.float32
bf16 = jnp.bfloat16


def split3(v):
    hi = v.astype(bf16)
    rest = v - hi.astype(f32)
    mid = rest.astype(bf16)
    low = (rest - mid.astype(f32)).astype(bf16)
    return hi, mid, low


def nt(a, b):
    return lax.dot_general(a, b, (((1,), (1,)), ((), ())), preferred_element_type=f32)


def nn(a, b):
    return lax.dot_general(a, b, (((1,), (0,)), ((), ())), preferred_element_type=f32)


def head_kernel(
    glob, local, weight, resid, tracks, a0, a1, a2, h_all, x_all, d_all, v_all, sums, q_ref, k_ref
):
    c = pl.program_id(0)

    @pl.when(c == 0)
    def _():
        sums[...] = jnp.zeros_like(sums)

        def first(s, carry):
            g = glob[s]
            gt = jnp.transpose(g.astype(f32))
            gt_low = gt.astype(bf16)
            t = tracks[pl.ds(s, 1), :]
            w = weight[pl.ds(s, 1), :]
            r = resid[pl.ds(s, 1), :]
            hot = lax.broadcasted_iota(jnp.int32, (TRK, PER), 0) == t
            a = local[s]
            wa = w * a
            zero = jnp.zeros((), f32)
            row = pl.ds(pl.multiple_of(s * BW, BW), BW)
            for j in range(LOC):
                spread = jnp.where(hot, wa[j : j + 1, :], zero).astype(bf16)
                h_all[row, j * TRK : (j + 1) * TRK] = nt(gt_low, spread).astype(bf16)
            terms = []
            for i in range(LOC):
                terms.append(wa[i : i + 1, :] * a)
            terms.append(wa * r)
            terms.append(jnp.zeros((4, PER), f32))
            stacked = jnp.concatenate(terms, axis=0)
            hot_low = jnp.where(hot, jnp.ones((), f32), zero).astype(bf16)
            hi, mid, low = split3(stacked)
            sums[...] += nt(hi, hot_low) + nt(mid, hot_low) + nt(low, hot_low)
            d_all[row, :] = nn((gt * w).astype(bf16), g)
            wr = jnp.broadcast_to((w * r).astype(bf16), (16, PER))
            v_all[pl.ds(pl.multiple_of(s * 8, 8), 8), :] = nn(wr, g)[:8]
            return carry

        lax.fori_loop(0, LAYERS, first, 0)

        one = jnp.ones((1, TRK), f32)
        nil = jnp.zeros((1, TRK), f32)
        rows = [
            [
                sums[4 * i + j : 4 * i + j + 1, :] + (one if i == j else nil)
                for j in range(LOC)
            ]
            for i in range(LOC)
        ]
        inv = [[one if i == j else nil for j in range(LOC)] for i in range(LOC)]
        for p in range(LOC):
            pivot = rows[p][p]
            scaled = [v / pivot for v in rows[p]]
            scaled_inv = [v / pivot for v in inv[p]]
            for o in range(LOC):
                if o != p:
                    factor = rows[o][p]
                    rows[o] = [u - factor * v for u, v in zip(rows[o], scaled)]
                    inv[o] = [u - factor * v for u, v in zip(inv[o], scaled_inv)]
            rows[p] = scaled
            inv[p] = scaled_inv
        for i in range(LOC):
            for j in range(LOC):
                k_ref[4 * i + j : 4 * i + j + 1, :] = inv[i][j]
        for j in range(LOC):
            q_ref[:, j * TRK : (j + 1) * TRK] = jnp.broadcast_to(
                sums[16 + j : 17 + j, :].astype(bf16), (16, TRK)
            )

        def second(s, carry):
            row = pl.ds(pl.multiple_of(s * BW, BW), BW)
            h = [h_all[row, l * TRK : (l + 1) * TRK].astype(f32) for l in range(LOC)]
            for j in range(LOC):
                x = h[0] * k_ref[j : j + 1, :]
                for l in range(1, LOC):
                    x = x + h[l] * k_ref[4 * l + j : 4 * l + j + 1, :]
                x_all[row, j * TRK : (j + 1) * TRK] = (-x).astype(bf16)
            v = pl.ds(pl.multiple_of(s * 8, 8), 8)
            v_all[v, :] = v_all[v, :] + nt(q_ref[...], x_all[row, :])[:8]
            return carry

        lax.fori_loop(0, LAYERS, second, 0)

    right = h_all[pl.ds(pl.multiple_of(c * 2 * BW, 2 * BW), 2 * BW), :]

    def gram(s2, carry):
        out = nt(x_all[pl.ds(pl.multiple_of(s2 * 4 * BW, 4 * BW), 4 * BW), :], right)
        for z in range(4):
            part = out[z * BW : (z + 1) * BW, :]
            a0[s2, z, 0] = part[0:88, :BW]
            a1[z, 0, s2, 0:40] = part[88:BW, :BW]
            a1[z, 0, s2, 40:88] = part[0:48, BW:]
            a2[0, s2, z, 0:80] = part[48:BW, BW:]
            a2[0, s2, z, 80:88] = v_all[pl.ds(pl.multiple_of((s2 * 4 + z) * 8, 8), 8), :]
        return carry

    lax.fori_loop(0, 4, gram, 0)
    s = 2 * c
    y, z = s // 4, s % 4
    base = pl.multiple_of(s * BW, BW)
    a0[y, z, 0] += d_all[pl.ds(base, 88), :]
    a1[z, 0, y, 0:40] += d_all[pl.ds(base + 88, 40), :]
    s = 2 * c + 1
    y, z = s // 4, s % 4
    base = pl.multiple_of(s * BW, BW)
    a1[z, 0, y, 40:88] += d_all[pl.ds(base, 48), :]
    a2[0, y, z, 0:80] += d_all[pl.ds(base + 48, 80), :]


def head(glob, local, weight, resid, tracks):
    def whole(*shape):
        return pl.BlockSpec(shape, lambda c: (0,) * len(shape))

    return pl.pallas_call(
        head_kernel,
        grid=(8,),
        in_specs=[
            whole(LAYERS, PER, BW),
            whole(LAYERS, LOC, PER),
            whole(LAYERS, PER),
            whole(LAYERS, PER),
            whole(LAYERS, PER),
        ],
        out_specs=(
            pl.BlockSpec((4, 4, 1, ROWS, BW), lambda c: (0, 0, c, 0, 0)),
            pl.BlockSpec((4, 1, 4, ROWS, BW), lambda c: (0, c, 0, 0, 0)),
            pl.BlockSpec((1, 4, 4, ROWS, BW), lambda c: (c, 0, 0, 0, 0)),
        ),
        out_shape=tuple(
            jax.ShapeDtypeStruct(tuple(SIZE[d] for d in order) + (ROWS, BW), f32)
            for order in ORDERS
        ),
        scratch_shapes=[
            pltpu.VMEM((LAYERS * BW, LOC * TRK), bf16),
            pltpu.VMEM((LAYERS * BW, LOC * TRK), bf16),
            pltpu.VMEM((LAYERS * BW, BW), f32),
            pltpu.VMEM((LAYERS * 8, BW), f32),
            pltpu.VMEM((24, TRK), f32),
            pltpu.VMEM((16, LOC * TRK), bf16),
            pltpu.VMEM((16, TRK), f32),
        ],
        compiler_params=pltpu.CompilerParams(
            dimension_semantics=("arbitrary",), vmem_limit_bytes=56 << 20
        ),
        name="head",
    )(glob, local, weight, resid, tracks)


def coords():
    r, c = lax.axis_index("row"), lax.axis_index("col")
    return {"y": r // 4, "z": r % 4, "X": c}


def moved(me, dim, offset, sign):
    if dim == "X":
        x, k = me["X"] // 2, me["X"] % 2
        dx, dk = offset // 2, offset % 2
        return ((x + 4 + sign * dx) % 4) * 2 + (k + dk) % 2
    return (me[dim] + 4 + sign * offset) % 4


def device(me, dim, place):
    at = dict(me)
    at[dim] = place
    return (at["y"] * 4 + at["z"], at["X"])


def offsets(dim):
    return WIDE if dim == "X" else RING


def exchange_kernel(a0, a1, a2, *refs):
    a = (a0, a1, a2)
    e, b, cc = refs[0:3], refs[3:6], refs[6:9]
    bounce2, bounce3 = refs[9:12], refs[12:15]
    s1, r1, s2, r2, s3, r3, lsem = refs[15:22]
    me = coords()
    sends = []
    locals_ = []

    def send(src, dst, ssem, rsem, dim, place):
        cp = pltpu.make_async_remote_copy(
            src_ref=src,
            dst_ref=dst,
            send_sem=ssem,
            recv_sem=rsem,
            device_id=device(me, dim, place),
            device_id_type=MESH,
        )
        cp.start()
        sends.append(cp)
        return cp

    def local(src, mid, dst, i):
        into = pltpu.make_async_copy(src, mid, lsem.at[i])
        into.start()
        into.wait()
        out = pltpu.make_async_copy(mid, dst, lsem.at[i])
        out.start()
        return out

    first = {}
    for step in range(7):
        for g, order in enumerate(ORDERS):
            d1 = order[0]
            offs = offsets(d1)
            if step < len(offs):
                o = offs[step]
                to = moved(me, d1, o, 1)
                first[g, o] = send(
                    a[g].at[to], b[g].at[me[d1]], s1.at[g, o], r1.at[g, o], d1, to
                )
    second = {}
    back2 = {}
    count = 0
    for step in range(8):
        for g, order in enumerate(ORDERS):
            d1, d2, _ = order
            offs = (0,) + offsets(d1)
            if step >= len(offs):
                continue
            o1 = offs[step]
            src1 = moved(me, d1, o1, -1)
            if o1:
                first[g, o1].wait_recv()
            for o2 in offsets(d2):
                to = moved(me, d2, o2, 1)
                src = b[g].at[src1, to] if o1 else a[g].at[me[d1], to]
                second[g, o1, o2] = send(
                    src, cc[g].at[me[d2], src1], s2.at[g, o1, o2], r2.at[g, o1, o2], d2, to
                )
            src = b[g].at[src1, me[d2]] if o1 else a[g].at[me[d1], me[d2]]
            back2[g, o1] = local(src, bounce2[g].at[o1], cc[g].at[me[d2], src1], count)
            count += 1
    third = []
    for step in range(8):
        for g, order in enumerate(ORDERS):
            d1, d2, d3 = order
            offs = (0,) + offsets(d2)
            if step >= len(offs):
                continue
            o2 = offs[step]
            src2 = moved(me, d2, o2, -1)
            for o1 in (0,) + offsets(d1):
                if o2:
                    second[g, o1, o2].wait_recv()
                else:
                    back2[g, o1].wait()
            for o3 in offsets(d3):
                to = moved(me, d3, o3, 1)
                third.append(
                    send(
                        cc[g].at[src2, :, to],
                        e[g].at[me[d3], src2],
                        s3.at[g, o2, o3],
                        r3.at[g, o2, o3],
                        d3,
                        to,
                    )
                )
            locals_.append(
                local(cc[g].at[src2, :, me[d3]], bounce3[g].at[o2], e[g].at[me[d3], src2], count)
            )
            count += 1
    for cp in locals_:
        cp.wait()
    for cp in third:
        cp.wait_recv()
    for cp in sends:
        cp.wait_send()


def exchange(a0, a1, a2):
    item = (ROWS, BW)
    sizes = [tuple(SIZE[d] for d in order) for order in ORDERS]
    shapes = (
        [jax.ShapeDtypeStruct((n3, n2, n1) + item, f32) for n1, n2, n3 in sizes]
        + [jax.ShapeDtypeStruct((n1, n2, n3) + item, f32) for n1, n2, n3 in sizes]
        + [jax.ShapeDtypeStruct((n2, n1, n3) + item, f32) for n1, n2, n3 in sizes]
    )
    any_ = pl.BlockSpec(memory_space=pl.ANY)
    out = pl.pallas_call(
        exchange_kernel,
        out_shape=tuple(shapes),
        in_specs=[any_] * 3,
        out_specs=(any_,) * 9,
        scratch_shapes=[pltpu.VMEM((n1, n3) + item, f32) for n1, n2, n3 in sizes]
        + [pltpu.VMEM((n2, n1) + item, f32) for n1, n2, n3 in sizes]
        + [
            pltpu.SemaphoreType.DMA((3, 8)),
            pltpu.SemaphoreType.DMA((3, 8)),
            pltpu.SemaphoreType.DMA((3, 8, 8)),
            pltpu.SemaphoreType.DMA((3, 8, 8)),
            pltpu.SemaphoreType.DMA((3, 8, 8)),
            pltpu.SemaphoreType.DMA((3, 8, 8)),
            pltpu.SemaphoreType.DMA((32,)),
        ],
        compiler_params=pltpu.CompilerParams(
            has_side_effects=True, vmem_limit_bytes=56 << 20
        ),
        name="exchange",
    )(a0, a1, a2)
    return out[:3]


def place_kernel(blocks, weak, e0, e1, e2, schur, product, rhs, diag):
    xb = pl.program_id(0)
    row, col = lax.axis_index("row"), lax.axis_index("col")

    @pl.when(xb == 0)
    def _():
        schur[...] = jnp.zeros_like(schur)
        rhs[...] = jnp.zeros_like(rhs)

    def bundle(i, carry):
        y, z = i // 4, i % 4
        b = i * 8 + xb
        k = blocks[b, row]
        l0 = pl.multiple_of(blocks[b, 2 * col] * BW, BW)
        l1 = pl.multiple_of(blocks[b, 2 * col + 1] * BW + GB * BW, BW)
        r = pl.multiple_of(k * BW, BW)
        schur[pl.ds(r, 88), pl.ds(l0, BW)] += e0[0, z, y]
        schur[pl.ds(r + 88, 40), pl.ds(l0, BW)] += e1[y, 0, z, 0:40]
        schur[pl.ds(r, 48), pl.ds(l1, BW)] += e1[y, 0, z, 40:88]
        schur[pl.ds(r + 48, 80), pl.ds(l1, BW)] += e2[z, y, 0, 0:80]
        rhs[pl.ds(k, 1), :] += e2[z, y, 0, 80:81]
        return carry

    lax.fori_loop(0, 16, bundle, 0)

    @pl.when(xb == 7)
    def _():
        w = weak[...]
        w_hi = w.astype(bf16)
        w_lo = (w - w_hi.astype(f32)).astype(bf16)

        def multiply(i, carry):
            r = pl.ds(pl.multiple_of(i * BW, BW), BW)
            v = schur[r, :]
            hi = v.astype(bf16)
            lo = (v - hi.astype(f32)).astype(bf16)
            product[r, :] = nn(hi, w_hi) + nn(hi, w_lo) + nn(lo, w_hi)
            return carry

        lax.fori_loop(0, GB, multiply, 0)
        side = pl.multiple_of((row % 2) * GB * BW, GB * BW)

        def corner(k, carry):
            at = pl.multiple_of(k * BW, BW)
            diag[k] = schur[pl.ds(at, BW), pl.ds(pl.multiple_of(side + at, BW), BW)]
            return carry

        lax.fori_loop(0, GB, corner, 0)

        @pl.when(col == row // 2)
        def _():
            schur[:, pl.ds(side, GB * BW)] = jnp.zeros((GB * BW, GB * BW), f32)


def place(blocks, weak, e0, e1, e2):
    def whole(*shape):
        return pl.BlockSpec(shape, lambda i: (0,) * len(shape))

    return pl.pallas_call(
        place_kernel,
        grid=(8,),
        in_specs=[
            pl.BlockSpec(memory_space=pltpu.SMEM),
            whole(2 * GB * BW, 64),
            pl.BlockSpec((1, 4, 4, ROWS, BW), lambda i: (i, 0, 0, 0, 0)),
            pl.BlockSpec((4, 1, 4, ROWS, BW), lambda i: (0, i, 0, 0, 0)),
            pl.BlockSpec((4, 4, 1, ROWS, BW), lambda i: (0, 0, i, 0, 0)),
        ],
        out_specs=(
            whole(GB * BW, 2 * GB * BW),
            whole(GB * BW, 64),
            whole(GB, BW),
            whole(GB, BW, BW),
        ),
        out_shape=(
            jax.ShapeDtypeStruct((GB * BW, 2 * GB * BW), f32),
            jax.ShapeDtypeStruct((GB * BW, 64), f32),
            jax.ShapeDtypeStruct((GB, BW), f32),
            jax.ShapeDtypeStruct((GB, BW, BW), f32),
        ),
        compiler_params=pltpu.CompilerParams(
            dimension_semantics=("arbitrary",), vmem_limit_bytes=56 << 20
        ),
        name="place",
    )(blocks, weak, e0, e1, e2)


def finish_kernel(product, diag, layer, weak, got, tile, ssem, rsem, tsend, trecv):
    me = coords()
    row = lax.axis_index("row")
    mine = me["X"]
    owner = row // 2
    copies = []
    for o in WIDE:
        to = moved(me, "X", o, 1)
        cp = pltpu.make_async_remote_copy(
            src_ref=product.at[pl.ds(pl.multiple_of(to * BW, BW), BW), :],
            dst_ref=got.at[o],
            send_sem=ssem.at[o],
            recv_sem=rsem.at[o],
            device_id=device(me, "X", to),
            device_id_type=MESH,
        )
        cp.start()
        copies.append(cp)

    def hand(o):
        to = moved(me, "X", o, 1)
        return pltpu.make_async_remote_copy(
            src_ref=diag.at[to],
            dst_ref=tile,
            send_sem=tsend.at[o],
            recv_sem=trecv,
            device_id=device(me, "X", to),
            device_id_type=MESH,
        )

    @pl.when(mine == owner)
    def _():
        for o in WIDE:
            hand(o).start()

    layer[...] = jnp.zeros_like(layer)
    here = pl.ds(pl.multiple_of(mine * BW, BW), BW)
    weak[...] = product[here, :]

    @pl.when(mine != owner)
    def _():
        hand(1).wait_recv()
        layer[here, :] = tile[...]

    @pl.when(mine == owner)
    def _():
        layer[here, :] = diag[mine]

    for cp in copies:
        cp.wait_recv()
    total = weak[...]
    for o in WIDE:
        total = total + got[o]
    weak[...] = total
    for cp in copies:
        cp.wait_send()

    @pl.when(mine == owner)
    def _():
        for o in WIDE:
            hand(o).wait_send()


def finish(product, diag):
    vmem = pl.BlockSpec(memory_space=pltpu.VMEM)
    return pl.pallas_call(
        finish_kernel,
        out_shape=(
            jax.ShapeDtypeStruct((GB * BW, BW), f32),
            jax.ShapeDtypeStruct((BW, 64), f32),
        ),
        in_specs=[vmem] * 2,
        out_specs=(vmem,) * 2,
        scratch_shapes=[
            pltpu.VMEM((8, BW, 64), f32),
            pltpu.VMEM((BW, BW), f32),
            pltpu.SemaphoreType.DMA((8,)),
            pltpu.SemaphoreType.DMA((8,)),
            pltpu.SemaphoreType.DMA((8,)),
            pltpu.SemaphoreType.DMA,
        ],
        compiler_params=pltpu.CompilerParams(has_side_effects=True),
        name="finish",
    )(product, diag)


def body(glob_derivs, local_derivs, weights, residuals, track_ids, module_blocks, weak_modes):
    a = head(glob_derivs[0], local_derivs[0], weights[0], residuals[0], track_ids[0])
    e = exchange(*a)
    schur, product, rhs, diag = place(module_blocks, weak_modes, *e)
    layer, weak = finish(product, diag)
    return schur, layer, rhs.reshape(GB * BW), weak


def solution(mesh):
    placed = (
        P(("row", "col"), None, None, None),
        P(("row", "col"), None, None, None),
        P(("row", "col"), None, None),
        P(("row", "col"), None, None),
        P(("row", "col"), None, None),
        P(),
        P("col", None),
    )
    return jax.shard_map(
        body,
        mesh=mesh,
        in_specs=placed,
        out_specs=(P("row", "col"), P("row", "col"), P("row"), P(("row", "col"), None)),
        check_vma=False,
    )
```

time: 478 us -> 287 us (0.60)
  Pallas kernels: 0 us -> 279 us
  waiting for transfers between devices: 265 us -> 0 us
  local copies, waits for them, and re-layouts: 79.2 us -> 5.44 us
  matrix products: 72.9 us -> 0 us
  starting transfers between devices: 33 us -> 0 us
  between operations: 14.4 us -> 0.66 us
  other arithmetic: 9.31 us -> 0 us
    pallas_call x0 -> x4, Pallas kernels: none -> 279 us  [the longest x1 208 us: exchange(): pl.pallas_call(exchange_kernel, out_shape=tuple(shapes), in_specs=[any_]...]
    all_to_all x2 -> x0, waiting for transfers between devices: 230 us -> none  [the longest x1 223 us: body(): lax.all_to_all(outgoing, ('row', 'col'), split_axis=0, concat_axis=0, til...]
    dot_general x13 -> x0, matrix products: 72.9 us -> none  [the longest x1 26.2 us: body(): jnp.einsum('bqkl,bqij->kiqlj', pairs, in_tiles, precision=lax.Precision.H...]
    all_to_all x2 -> x0, starting transfers between devices: 32.9 us -> none  [the longest x1 21.8 us: body(): lax.all_to_all(vec_out, ('row', 'col'), split_axis=0, concat_axis=0, tile...]
    reduce_scatter x1 -> x0, waiting for transfers between devices: 31.4 us -> none  [body(): lax.psum_scatter(product, 'col', scatter_dimension=0, tiled=True)]
    mul x7 -> x0, local copies, waits for them, and re-layouts: 22.7 us -> none  [the longest x5 15.1 us: bundle_terms(): h_wide[..., lidx:lidx + 1] * jnp.transpose(kinv[lidx])[None, None]]
    reshape x2 -> x0, local copies, waits for them, and re-layouts: 18.6 us -> none  [the longest x1 9.35 us: body(): placed.reshape(GB * BW, groups * GB * BW)]
    sub x1 -> x0, local copies, waits for them, and re-layouts: 17.6 us -> none  [bundle_terms(): jnp.eye(layers, dtype=f32)[:, :, None, None] * diag_tiles[:, None, :, :]]
  transfers between devices with their start and end apart: 4 -> 0, of which waited for: 4 -> 0; matrix products, arithmetic and copies ran while one was open for 12% -> 0% of each run, Pallas kernels for 0% -> 0%
where the time goes in v1:
time: 287 us; the launch traced here: 285 us
  Pallas kernels  279 us (97%)
  local copies, waits for them, and re-layouts  5.44 us (2%)
    pallas_call x1, Pallas kernels, exchange(): pl.pallas_call(exchange_kernel, out_shape=tuple(shapes), in_specs=[any_]...  208 us
    pallas_call x1, Pallas kernels, head(): pl.pallas_call(head_kernel, grid=(8,), in_specs=[whole(LAYERS, PER, BW),...  30.3 us
    pallas_call x1, Pallas kernels, finish(): pl.pallas_call(finish_kernel, out_shape=(jax.ShapeDtypeStruct((GB * BW, B...  21.7 us
    pallas_call x1, Pallas kernels, place(): pl.pallas_call(place_kernel, grid=(8,), in_specs=[pl.BlockSpec(memory_spa...  19.7 us

profile of v1, /device:TPU:17, one launch (start us, length us, event | category | flops | bytes accessed | tf_op | source)
XLA Modules:
  0.0 285.4 jit_solution(7999201731217499045)
XLA Ops:
  0.6 30.3 %head.1 = (f32[4,4,8,88,128]{4,3,2,1,0:T(8,128)}, f32[4,8,4,88,128]{4,3,2,1,0:T(8,128)}, f32[8,4,4,88,128]{4,3,2,1,0:T(8,128)}) custom-call(bf16[16,256,128]{2,1,0:T(8,128)(2,1)} %bitcast.6, f32[16,4,256]{2,1,0:T(4,128)} %bitcast.7, f32[16,256]{1,0:T(8,128)} %bitcast.8, f32[16,256]{1,0:T(8,128)} %bitcast.9, s32[16,256]{1,0:T(8,128)} %bitcast.10), custom_call_target="tpu_custom_call" | custom-call | tf_op jit(solution)/shard_map/head/pallas_call | solution.py:155
  30.9 0.0 copy-start
  30.9 0.0 copy-start.1
  30.9 207.6 %exchange.1 = (f32[8,4,4,88,128]{4,3,2,1,0:T(8,128)}, f32[4,8,4,88,128]{4,3,2,1,0:T(8,128)}, f32[4,4,8,88,128]{4,3,2,1,0:T(8,128)}, f32[4,4,8,88,128]{4,3,2,1,0:...) custom-call(f32[4,4,8,88,128]{4,3,2,1,0:T(8,128)} %get-tuple-element, ...), custom_call_target="tpu_custom_call" | custom-call | tf_op jit(solution)/shard_map/exchange/pallas_call | solution.py:323
  238.6 0.0 copy-done
  238.6 1.3 copy.12.weak
  239.9 0.0 copy-done.1
  239.9 0.7 copy.11.blocks
  240.6 19.7 %place.1 = (f32[1024,2048]{1,0:T(8,128)}, f32[1024,64]{1,0:T(8,128)}, f32[8,128]{1,0:T(8,128)}, f32[8,128,128]{2,1,0:T(8,128)}) custom-call(s32[128,16]{1,0:T(8,128)} %copy.11.blocks, f32[2048,64]{1,0:T(8,128)} %copy.12.weak, f32[8,4,4,88,128]{4,3,2,1,0:T(8,128)} %get-tuple-element.19.e0, f32[4,8,4,88,128]{4,3,2,1,0:T(8,128)} %get-tuple-element.20.e1, ...), custom_call_target="tpu_custom_call" | custom-call | tf_op jit(solution)/shard_map/place/pallas_call | solution.py:405
  260.3 21.7 %finish.1 = (f32[1024,128]{1,0:T(8,128)}, f32[128,64]{1,0:T(8,128)}) custom-call(f32[1024,64]{1,0:T(8,128)} %get-tuple-element.23.product, f32[8,128,128]{2,1,0:T(8,128)} %get-tuple-element.24.diag), custom_call_target="tpu_custom_call" | custom-call | tf_op jit(solution)/shard_map/finish/pallas_call | solution.py:499
  282.0 1.5 copy.13
  283.5 1.9 copy.15
Async XLA Ops:
  30.9 207.6 %copy-start = (f32[2048,64]{0,1:T(8,128)S(1)}, f32[2048,64]{0,1:T(8,128)}, u32[]{:S(2)}) copy-start(f32[2048,64]{0,1:T(8,128)} %param.13) | copy-start | bytes 1572868
  30.9 208.9 %copy-start.1 = (s32[128,16]{0,1:T(8,128)S(1)}, s32[128,16]{0,1:T(8,128)}, u32[]{:S(2)}) copy-start(s32[128,16]{0,1:T(8,128)} %param.12) | copy-start | bytes 24580

commit v2 on v1

v2 whole, which is shorter than its diff:
```python
import functools

import jax
import jax.numpy as jnp
from jax import lax
from jax.experimental import pallas as pl
from jax.experimental.pallas import tpu as pltpu
from jax.sharding import PartitionSpec as P

BW = 128
GB = 8
LOC = 4
TRK = 256
LAYERS = 16
PER = 256
ROWS = (88, 88, 80)
SIZE = {"y": 4, "z": 4, "X": 8}
ORDERS = (("y", "z", "X"), ("z", "X", "y"), ("X", "y", "z"))
RING = (1, 3, 2)
WIDE = (2, 6, 3, 7, 4, 5, 1)
CHUNKS = (2, 6, 3, 7, 0, 4, 5, 1)
MESH = pl.DeviceIdType.MESH
f32 = jnp.float32
bf16 = jnp.bfloat16


def split3(v):
    hi = v.astype(bf16)
    rest = v - hi.astype(f32)
    mid = rest.astype(bf16)
    low = (rest - mid.astype(f32)).astype(bf16)
    return hi, mid, low


def nt(a, b):
    return lax.dot_general(a, b, (((1,), (1,)), ((), ())), preferred_element_type=f32)


def nn(a, b):
    return lax.dot_general(a, b, (((1,), (0,)), ((), ())), preferred_element_type=f32)


def local_terms(glob, local, weight, resid, tracks, h_all, x_all, d_all, v_all, sums, q_ref, k_ref):
    sums[...] = jnp.zeros_like(sums)

    def first(s, carry):
        g = glob[s]
        gt = jnp.transpose(g.astype(f32))
        gt_low = gt.astype(bf16)
        t = tracks[pl.ds(s, 1), :]
        w = weight[pl.ds(s, 1), :]
        r = resid[pl.ds(s, 1), :]
        hot = lax.broadcasted_iota(jnp.int32, (TRK, PER), 0) == t
        a = local[s]
        wa = w * a
        zero = jnp.zeros((), f32)
        row = pl.ds(pl.multiple_of(s * BW, BW), BW)
        for j in range(LOC):
            spread = jnp.where(hot, wa[j : j + 1, :], zero).astype(bf16)
            h_all[row, j * TRK : (j + 1) * TRK] = nt(gt_low, spread).astype(bf16)
        terms = []
        for i in range(LOC):
            terms.append(wa[i : i + 1, :] * a)
        terms.append(wa * r)
        terms.append(jnp.zeros((4, PER), f32))
        stacked = jnp.concatenate(terms, axis=0)
        hot_low = jnp.where(hot, jnp.ones((), f32), zero).astype(bf16)
        hi, mid, low = split3(stacked)
        sums[...] += nt(hi, hot_low) + nt(mid, hot_low) + nt(low, hot_low)
        d_all[row, :] = nn((gt * w).astype(bf16), g)
        wr = jnp.broadcast_to((w * r).astype(bf16), (16, PER))
        v_all[s // 4, s % 4] = nn(wr, g)[:8]
        return carry

    lax.fori_loop(0, LAYERS, first, 0)

    one = jnp.ones((1, TRK), f32)
    nil = jnp.zeros((1, TRK), f32)
    rows = [
        [sums[4 * i + j : 4 * i + j + 1, :] + (one if i == j else nil) for j in range(LOC)]
        for i in range(LOC)
    ]
    inv = [[one if i == j else nil for j in range(LOC)] for i in range(LOC)]
    for p in range(LOC):
        pivot = rows[p][p]
        scaled = [v / pivot for v in rows[p]]
        scaled_inv = [v / pivot for v in inv[p]]
        for o in range(LOC):
            if o != p:
                factor = rows[o][p]
                rows[o] = [u - factor * v for u, v in zip(rows[o], scaled)]
                inv[o] = [u - factor * v for u, v in zip(inv[o], scaled_inv)]
        rows[p] = scaled
        inv[p] = scaled_inv
    for i in range(LOC):
        for j in range(LOC):
            k_ref[4 * i + j : 4 * i + j + 1, :] = inv[i][j]
    for j in range(LOC):
        q_ref[:, j * TRK : (j + 1) * TRK] = jnp.broadcast_to(
            sums[16 + j : 17 + j, :].astype(bf16), (16, TRK)
        )

    def second(s, carry):
        row = pl.ds(pl.multiple_of(s * BW, BW), BW)
        h = [h_all[row, l * TRK : (l + 1) * TRK].astype(f32) for l in range(LOC)]
        for j in range(LOC):
            x = h[0] * k_ref[j : j + 1, :]
            for l in range(1, LOC):
                x = x + h[l] * k_ref[4 * l + j : 4 * l + j + 1, :]
            x_all[row, j * TRK : (j + 1) * TRK] = (-x).astype(bf16)
        v_all[s // 4, s % 4] = v_all[s // 4, s % 4] + nt(q_ref[...], x_all[row, :])[:8]
        return carry

    lax.fori_loop(0, LAYERS, second, 0)


def tiles_for(c, a0, a1, a2, h_all, x_all, d_all):
    right = h_all[pl.ds(pl.multiple_of(c * 2 * BW, 2 * BW), 2 * BW), :]

    def gram(y, carry):
        out = nt(x_all[pl.ds(pl.multiple_of(y * 4 * BW, 4 * BW), 4 * BW), :], right)
        for z in range(4):
            part = out[z * BW : (z + 1) * BW, :]
            a0[y, z, c] = part[0:88, :BW]
            a1[z, c, y, 0:40] = part[88:BW, :BW]
            a1[z, c, y, 40:88] = part[0:48, BW:]
            a2[c, y, z] = part[48:BW, BW:]
        return carry

    lax.fori_loop(0, 4, gram, 0)
    s = 2 * c
    y, z = s // 4, s % 4
    base = pl.multiple_of(s * BW, BW)
    a0[y, z, c] += d_all[pl.ds(base, 88), :]
    a1[z, c, y, 0:40] += d_all[pl.ds(base + 88, 40), :]
    base = pl.multiple_of(s * BW + BW, BW)
    a1[z + 1, c, y, 40:88] += d_all[pl.ds(base, 48), :]
    a2[c, y, z + 1] += d_all[pl.ds(base + 48, 80), :]


def coords():
    r, c = lax.axis_index("row"), lax.axis_index("col")
    return {"y": r // 4, "z": r % 4, "X": c}


def moved(me, dim, offset, sign):
    if dim == "X":
        x, k = me["X"] // 2, me["X"] % 2
        dx, dk = offset // 2, offset % 2
        return ((x + 4 + sign * dx) % 4) * 2 + (k + dk) % 2
    return (me[dim] + 4 + sign * offset) % 4


def device(me, dim, place):
    at = dict(me)
    at[dim] = place
    return (at["y"] * 4 + at["z"], at["X"])


def offsets(dim):
    return WIDE if dim == "X" else RING


def greet(me, dims):
    barrier = pltpu.get_barrier_semaphore()
    count = 0
    for dim in dims:
        for o in offsets(dim):
            pl.semaphore_signal(
                barrier,
                inc=1,
                device_id=device(me, dim, moved(me, dim, o, 1)),
                device_id_type=MESH,
            )
            count += 1
    return barrier, count


def exchange_kernel(glob, local, weight, resid, tracks, *refs):
    e, v_out, b, cc = refs[0:3], refs[3], refs[4:7], refs[7:10]
    a = refs[10:13]
    bounce2, bounce3 = refs[13:16], refs[16:19]
    h_all, x_all, d_all, v_all, v_mid, sums, q_ref, k_ref = refs[19:27]
    s1, r1, s2, r2, s3, r3, lsem, vs, vr = refs[27:36]
    me = coords()
    barrier, count = greet(me, ("y", "z", "X"))
    local_terms(
        glob, local, weight, resid, tracks, h_all, x_all, d_all, v_all, sums, q_ref, k_ref
    )
    pl.semaphore_wait(barrier, count)
    sends = []

    def send(src, dst, ssem, rsem, dim, place):
        cp = pltpu.make_async_remote_copy(
            src_ref=src,
            dst_ref=dst,
            send_sem=ssem,
            recv_sem=rsem,
            device_id=device(me, dim, place),
            device_id_type=MESH,
        )
        cp.start()
        sends.append(cp)
        return cp

    pending = []
    count = [0]

    def local_copy(src, mid, dst, done):
        into = pltpu.make_async_copy(src, mid, lsem.at[count[0]])
        out = pltpu.make_async_copy(mid, dst, lsem.at[count[0]])
        count[0] += 1
        into.start()
        pending.append((into, out))
        done.append(out)

    def flush():
        for into, out in pending:
            into.wait()
            out.start()
        pending.clear()

    fifth = {}

    def stage1(j):
        o = CHUNKS[j]
        c = moved(me, "X", o, 1)
        for oo in RING:
            to = moved(me, "y", oo, 1)
            send(a[0].at[to, :, c], b[0].at[me["y"], :, c], s1.at[0, oo, j], r1.at[0, oo, j], "y", to)
            to = moved(me, "z", oo, 1)
            send(a[1].at[to, c], b[1].at[me["z"], c], s1.at[1, oo, j], r1.at[1, oo, j], "z", to)
        if o:
            send(a[2].at[c], b[2].at[me["X"]], s1.at[2, o, 0], r1.at[2, o, 0], "X", c)

    for j, o in enumerate(CHUNKS):
        tiles_for(moved(me, "X", o, 1), *a, h_all, x_all, d_all)
        if j:
            stage1(j - 1)
    for oo in RING:
        to = moved(me, "y", oo, 1)
        fifth[oo] = send(v_all.at[to], v_mid.at[me["y"]], vs.at[0, oo], vr.at[0, oo], "y", to)
    v_mid[me["y"]] = v_all[me["y"]]
    stage1(7)

    def arrived1(g, o):
        src = moved(me, ORDERS[g][0], o, -1)
        if g == 2:
            pltpu.make_async_copy(b[2].at[src], b[2].at[src], r1.at[2, o, 0]).wait()
            return
        for j, oc in enumerate(CHUNKS):
            c = moved(me, "X", oc, 1)
            ref = b[0].at[src, :, c] if g == 0 else b[1].at[src, c]
            pltpu.make_async_copy(ref, ref, r1.at[g, o, j]).wait()

    second = {}
    back2 = {}
    for step in range(8):
        for g, order in enumerate(ORDERS):
            d1, d2, _ = order
            offs = (0,) + offsets(d1)
            if step >= len(offs):
                continue
            o1 = offs[step]
            src1 = moved(me, d1, o1, -1)
            if o1:
                arrived1(g, o1)
            for o2 in offsets(d2):
                to = moved(me, d2, o2, 1)
                src = b[g].at[src1, to] if o1 else a[g].at[me[d1], to]
                second[g, o1, o2] = send(
                    src, cc[g].at[me[d2], src1], s2.at[g, o1, o2], r2.at[g, o1, o2], d2, to
                )
            flush()
            done = back2.setdefault(g, [])
            if o1:
                local_copy(b[g].at[src1, me[d2]], bounce2[g].at[o1], cc[g].at[me[d2], src1], done)
            else:
                out = pltpu.make_async_copy(
                    a[g].at[me[d1], me[d2]], cc[g].at[me[d2], src1], lsem.at[count[0]]
                )
                count[0] += 1
                out.start()
                done.append(out)
    for oo in RING:
        fifth[oo].wait_recv()
    v_last = {}
    for oo in RING:
        to = moved(me, "z", oo, 1)
        v_last[oo] = send(v_mid.at[:, to], v_out.at[me["z"]], vs.at[1, oo], vr.at[1, oo], "z", to)
    v_out[me["z"]] = v_mid[:, me["z"]]
    flush()
    third = []
    last = []
    for step in range(8):
        for g, order in enumerate(ORDERS):
            d1, d2, d3 = order
            offs = (0,) + offsets(d2)
            if step >= len(offs):
                continue
            o2 = offs[step]
            src2 = moved(me, d2, o2, -1)
            if o2:
                for o1 in (0,) + offsets(d1):
                    second[g, o1, o2].wait_recv()
            else:
                for out in back2[g]:
                    out.wait()
            for o3 in offsets(d3):
                to = moved(me, d3, o3, 1)
                third.append(
                    send(
                        cc[g].at[src2, :, to],
                        e[g].at[me[d3], src2],
                        s3.at[g, o2, o3],
                        r3.at[g, o2, o3],
                        d3,
                        to,
                    )
                )
            flush()
            local_copy(cc[g].at[src2, :, me[d3]], bounce3[g].at[o2], e[g].at[me[d3], src2], last)
    flush()
    for oo in RING:
        v_last[oo].wait_recv()
    for cp in last:
        cp.wait()
    for cp in third:
        cp.wait_recv()
    for cp in sends:
        cp.wait_send()


def exchange(glob, local, weight, resid, tracks):
    sizes = [tuple(SIZE[d] for d in order) for order in ORDERS]
    items = [(rows, BW) for rows in ROWS]
    both = list(zip(sizes, items))
    shapes = (
        [jax.ShapeDtypeStruct((n3, n2, n1) + it, f32) for (n1, n2, n3), it in both]
        + [jax.ShapeDtypeStruct((4, 4, 8, BW), f32)]
        + [jax.ShapeDtypeStruct((n1, n2, n3) + it, f32) for (n1, n2, n3), it in both]
        + [jax.ShapeDtypeStruct((n2, n1, n3) + it, f32) for (n1, n2, n3), it in both]
    )
    any_ = pl.BlockSpec(memory_space=pl.ANY)
    vmem = pl.BlockSpec(memory_space=pltpu.VMEM)
    out = pl.pallas_call(
        exchange_kernel,
        out_shape=tuple(shapes),
        in_specs=[vmem] * 5,
        out_specs=(any_,) * 3 + (vmem,) + (any_,) * 6,
        scratch_shapes=[pltpu.VMEM(n + it, f32) for n, it in both]
        + [pltpu.VMEM((n1, n3) + it, f32) for (n1, n2, n3), it in both]
        + [pltpu.VMEM((n2, n1) + it, f32) for (n1, n2, n3), it in both]
        + [
            pltpu.VMEM((LAYERS * BW, LOC * TRK), bf16),
            pltpu.VMEM((LAYERS * BW, LOC * TRK), bf16),
            pltpu.VMEM((LAYERS * BW, BW), f32),
            pltpu.VMEM((4, 4, 8, BW), f32),
            pltpu.VMEM((4, 4, 8, BW), f32),
            pltpu.VMEM((24, TRK), f32),
            pltpu.VMEM((16, LOC * TRK), bf16),
            pltpu.VMEM((16, TRK), f32),
            pltpu.SemaphoreType.DMA((3, 8, 8)),
            pltpu.SemaphoreType.DMA((3, 8, 8)),
            pltpu.SemaphoreType.DMA((3, 8, 8)),
            pltpu.SemaphoreType.DMA((3, 8, 8)),
            pltpu.SemaphoreType.DMA((3, 8, 8)),
            pltpu.SemaphoreType.DMA((3, 8, 8)),
            pltpu.SemaphoreType.DMA((32,)),
            pltpu.SemaphoreType.DMA((2, 4)),
            pltpu.SemaphoreType.DMA((2, 4)),
        ],
        compiler_params=pltpu.CompilerParams(
            collective_id=0, has_side_effects=True, vmem_limit_bytes=60 << 20
        ),
        name="exchange",
    )(glob, local, weight, resid, tracks)
    return out[:4]


def place_kernel(blocks, weak, e0, e1, e2, vec, schur, product, rhs, diag, acc, w_ref, p_ref, sem):
    xb = pl.program_id(0)
    row, col = lax.axis_index("row"), lax.axis_index("col")

    @pl.when(xb == 0)
    def _():
        acc[...] = jnp.zeros_like(acc)
        rhs[...] = jnp.zeros_like(rhs)

        def term(i, carry):
            k = blocks[row, i * 8 + col]
            rhs[pl.ds(k, 1), :] += vec[i % 4, i // 4, 0:1]
            return carry

        lax.fori_loop(0, 16, term, 0)

    def bundle(i, carry):
        y, z = i // 4, i % 4
        b = i * 8 + xb
        l0 = pl.multiple_of(blocks[2 * col, b] * BW, BW)
        l1 = pl.multiple_of(blocks[2 * col + 1, b] * BW + GB * BW, BW)
        r = pl.multiple_of(blocks[row, b] * BW, BW)
        acc[pl.ds(r, 88), pl.ds(l0, BW)] += e0[0, z, y]
        acc[pl.ds(r + 88, 40), pl.ds(l0, BW)] += e1[y, 0, z, 0:40]
        acc[pl.ds(r, 48), pl.ds(l1, BW)] += e1[y, 0, z, 40:88]
        acc[pl.ds(r + 48, 80), pl.ds(l1, BW)] += e2[z, y, 0]
        return carry

    lax.fori_loop(0, 16, bundle, 0)

    @pl.when(xb == 7)
    def _():
        w = weak[...]
        w_hi = w.astype(bf16)
        w_ref[0:64, :] = w_hi
        w_ref[64:128, :] = (w - w_hi.astype(f32)).astype(bf16)
        p_ref[...] = jnp.zeros_like(p_ref)

        def copy_out(ch):
            cols = pl.ds(pl.multiple_of(ch * 256, 256), 256)
            return pltpu.make_async_copy(acc.at[:, cols], schur.at[:, cols], sem.at[ch])

        def chunk(ch, carry):
            cols = pl.ds(pl.multiple_of(ch * 256, 256), 256)
            wc = w_ref[:, cols]

            def multiply(i, carry):
                r = pl.ds(pl.multiple_of(i * 256, 256), 256)
                v = acc[r, cols]
                hi = v.astype(bf16)
                lo = (v - hi.astype(f32)).astype(bf16)
                p_ref[r, :] += nt(hi, wc) + nt(lo, wc)
                return carry

            lax.fori_loop(0, 4, multiply, 0)

            @pl.when(ch // 4 == row % 2)
            def _():
                for m in range(2):
                    k = 2 * (ch % 4) + m
                    diag[k] = acc[
                        pl.ds(pl.multiple_of(k * BW, BW), BW),
                        pl.ds(pl.multiple_of(ch * 256 + m * BW, BW), BW),
                    ]

                @pl.when(col == row // 2)
                def _():
                    acc[:, cols] = jnp.zeros((GB * BW, 256), f32)

            copy_out(ch).start()
            return carry

        lax.fori_loop(0, 8, chunk, 0)
        for k in range(GB):
            pt = jnp.transpose(p_ref[k * BW : (k + 1) * BW, :])
            product[k] = pt[0:64] + pt[64:128]
        for ch in range(8):
            copy_out(ch).wait()


def place(blocks, weak, e0, e1, e2, vec):
    def whole(*shape):
        return pl.BlockSpec(shape, lambda i: (0,) * len(shape))

    r0, r1, r2 = ROWS
    return pl.pallas_call(
        place_kernel,
        grid=(8,),
        in_specs=[
            pl.BlockSpec(memory_space=pltpu.SMEM),
            whole(64, 2 * GB * BW),
            pl.BlockSpec((1, 4, 4, r0, BW), lambda i: (i, 0, 0, 0, 0)),
            pl.BlockSpec((4, 1, 4, r1, BW), lambda i: (0, i, 0, 0, 0)),
            pl.BlockSpec((4, 4, 1, r2, BW), lambda i: (0, 0, i, 0, 0)),
            whole(4, 4, 8, BW),
        ],
        out_specs=(
            pl.BlockSpec(memory_space=pl.ANY),
            whole(GB, 64, BW),
            whole(GB, BW),
            whole(GB, BW, BW),
        ),
        out_shape=(
            jax.ShapeDtypeStruct((GB * BW, 2 * GB * BW), f32),
            jax.ShapeDtypeStruct((GB, 64, BW), f32),
            jax.ShapeDtypeStruct((GB, BW), f32),
            jax.ShapeDtypeStruct((GB, BW, BW), f32),
        ),
        scratch_shapes=[
            pltpu.VMEM((GB * BW, 2 * GB * BW), f32),
            pltpu.VMEM((BW, 2 * GB * BW), bf16),
            pltpu.VMEM((GB * BW, BW), f32),
            pltpu.SemaphoreType.DMA((8,)),
        ],
        compiler_params=pltpu.CompilerParams(
            dimension_semantics=("arbitrary",), vmem_limit_bytes=56 << 20
        ),
        name="place",
    )(blocks, weak, e0, e1, e2, vec)


def finish_kernel(product, diag, part, weak, tile, rhs, got, got_r, ssem, rsem, tsend, trecv):
    me = coords()
    row = lax.axis_index("row")
    mine = me["X"]
    owner = row // 2
    barrier, count = greet(me, ("X",))
    pl.semaphore_wait(barrier, count)
    copies = []
    for o in WIDE:
        to = moved(me, "X", o, 1)
        for i, (src, dst) in enumerate(((product.at[to], got.at[o]), (part, got_r.at[o]))):
            cp = pltpu.make_async_remote_copy(
                src_ref=src,
                dst_ref=dst,
                send_sem=ssem.at[i, o],
                recv_sem=rsem.at[i, o],
                device_id=device(me, "X", to),
                device_id_type=MESH,
            )
            cp.start()
            copies.append(cp)

    def hand(o):
        to = moved(me, "X", o, 1)
        return pltpu.make_async_remote_copy(
            src_ref=diag.at[to],
            dst_ref=tile,
            send_sem=tsend.at[o],
            recv_sem=trecv,
            device_id=device(me, "X", to),
            device_id_type=MESH,
        )

    @pl.when(mine == owner)
    def _():
        for o in WIDE:
            hand(o).start()
        tile[...] = diag[mine]

    for cp in copies:
        cp.wait_recv()
    total = product[mine]
    total_r = part[...]
    for o in WIDE:
        total = total + got[o]
        total_r = total_r + got_r[o]
    weak[...] = total
    rhs[...] = total_r
    for cp in copies:
        cp.wait_send()

    @pl.when(mine != owner)
    def _():
        hand(1).wait_recv()

    @pl.when(mine == owner)
    def _():
        for o in WIDE:
            hand(o).wait_send()


def finish(product, diag, part):
    vmem = pl.BlockSpec(memory_space=pltpu.VMEM)
    return pl.pallas_call(
        finish_kernel,
        out_shape=(
            jax.ShapeDtypeStruct((64, BW), f32),
            jax.ShapeDtypeStruct((BW, BW), f32),
            jax.ShapeDtypeStruct((GB, BW), f32),
        ),
        in_specs=[vmem] * 3,
        out_specs=(vmem,) * 3,
        scratch_shapes=[
            pltpu.VMEM((8, 64, BW), f32),
            pltpu.VMEM((8, GB, BW), f32),
            pltpu.SemaphoreType.DMA((2, 8)),
            pltpu.SemaphoreType.DMA((2, 8)),
            pltpu.SemaphoreType.DMA((8,)),
            pltpu.SemaphoreType.DMA,
        ],
        compiler_params=pltpu.CompilerParams(collective_id=1, has_side_effects=True),
        name="finish",
    )(product, diag, part)


def body(glob_derivs, local_derivs, weights, residuals, track_ids, module_blocks, weak_modes):
    e = exchange(glob_derivs[0], local_derivs[0], weights[0], residuals[0], track_ids[0])
    schur, product, part, diag = place(module_blocks.T, weak_modes.T, *e)
    weak, tile, rhs = finish(product, diag, part)
    here = jnp.arange(GB)[:, None, None] == lax.axis_index("col")
    layer = jnp.where(here, tile[None], jnp.zeros((), f32)).reshape(GB * BW, BW)
    return schur, layer, rhs.reshape(GB * BW), weak.T


def solution(mesh):
    placed = (
        P(("row", "col"), None, None, None),
        P(("row", "col"), None, None, None),
        P(("row", "col"), None, None),
        P(("row", "col"), None, None),
        P(("row", "col"), None, None),
        P(),
        P("col", None),
    )
    return jax.shard_map(
        body,
        mesh=mesh,
        in_specs=placed,
        out_specs=(P("row", "col"), P("row", "col"), P("row"), P(("row", "col"), None)),
        check_vma=False,
    )
```

time: 287 us -> 255 us (0.89)
  Pallas kernels: 279 us -> 249 us
    pallas_call x3 -> x2, Pallas kernels: 260 us -> 228 us  [the longest x1 214 us: exchange(): pl.pallas_call(exchange_kernel, out_shape=tuple(shapes), in_specs=[vmem]...]
where the time goes in v2:
time: 255 us; the launch traced here: 254 us
  Pallas kernels  249 us (98%)
  local copies, waits for them, and re-layouts  2.72 us (1%)
    pallas_call x1, Pallas kernels, exchange(): pl.pallas_call(exchange_kernel, out_shape=tuple(shapes), in_specs=[vmem]...  214 us
    pallas_call x1, Pallas kernels, place(): pl.pallas_call(place_kernel, grid=(8,), in_specs=[pl.BlockSpec(memory_spa...  20.8 us
    pallas_call x1, Pallas kernels, finish(): pl.pallas_call(finish_kernel, out_shape=(jax.ShapeDtypeStruct((64, BW), f...  13.9 us

profile of v2, /device:TPU:17, one launch (start us, length us, event | category | flops | bytes accessed | tf_op | source)
XLA Modules:
  0.0 254.1 jit_solution(2963406641029139793)
XLA Ops:
  0.6 214.1 %exchange.1 = (f32[8,4,4,88,128]{4,3,2,1,0:T(8,128)}, f32[4,8,4,88,128]{4,3,2,1,0:T(8,128)}, f32[4,4,8,80,128]{4,3,2,1,0:T(8,128)}, f32[4,4,8,128]{3,2,1,0:T(8,1...) custom-call(bf16[16,256,128]{2,1,0:T(8,128)(2,1)} %bitcast.13, ...), custom_call_target="tpu_custom_call" | custom-call | tf_op jit(solution)/shard_map/exchange/pallas_call | solution.py:346
  214.7 20.8 %place.1 = (f32[1024,2048]{1,0:T(8,128)}, f32[8,64,128]{2,1,0:T(8,128)}, f32[8,128]{1,0:T(8,128)}, f32[8,128,128]{2,1,0:T(8,128)}) custom-call(s32[16,128]{1,0:T(8,128)} %bitcast.20, f32[64,2048]{1,0:T(8,128)} %bitcast.14, f32[8,4,4,88,128]{4,3,2,1,0:T(8,128)} %get-tuple-element.15.e0, f32[4,8,4,88,128]{4,3,2,1,0:T(8,128)} %get-tuple-element.16.e1, ...), custom_call_target="tpu_custom_call" | custom-call | tf_op jit(solution)/shard_map/place/pallas_call | solution.py:466
  235.6 13.9 %finish.1 = (f32[64,128]{1,0:T(8,128)}, f32[128,128]{1,0:T(8,128)}, f32[8,128]{1,0:T(8,128)}) custom-call(f32[8,64,128]{2,1,0:T(8,128)} %get-tuple-element.20.product, f32[8,128,128]{2,1,0:T(8,128)} %get-tuple-element.21.diag, f32[8,128]{1,0:T(8,128)} %get-tuple-element.22.part), custom_call_target="tpu_custom_call" | custom-call | tf_op jit(solution)/shard_map/finish/pallas_call | solution.py:565
  249.5 0.1 broadcast_bitcast_fusion
  249.6 1.8 bitcast_select_fusion
  251.4 1.3 copy.13
  252.7 1.4 copy.14
  (1 shorter events, 0.0 us)

commit v3 on v2

--- a/solution.py
+++ b/solution.py
@@ -181,14 +181,13 @@
     a = refs[10:13]
     bounce2, bounce3 = refs[13:16], refs[16:19]
     h_all, x_all, d_all, v_all, v_mid, sums, q_ref, k_ref = refs[19:27]
-    s1, r1, s2, r2, s3, r3, lsem, vs, vr = refs[27:36]
+    ssem, r1, r2, r3, into_sem, out_sem, v_sem = refs[27:34]
     me = coords()
     barrier, count = greet(me, ("y", "z", "X"))
     local_terms(
         glob, local, weight, resid, tracks, h_all, x_all, d_all, v_all, sums, q_ref, k_ref
     )
     pl.semaphore_wait(barrier, count)
-    sends = []
 
     def send(src, dst, ssem, rsem, dim, place):
         cp = pltpu.make_async_remote_copy(
@@ -200,19 +199,16 @@
             device_id_type=MESH,
         )
         cp.start()
-        sends.append(cp)
-        return cp
+
+    def wait_for(ref, sem):
+        pltpu.make_async_copy(ref, ref, sem).wait()
 
     pending = []
-    count = [0]
-
-    def local_copy(src, mid, dst, done):
-        into = pltpu.make_async_copy(src, mid, lsem.at[count[0]])
-        out = pltpu.make_async_copy(mid, dst, lsem.at[count[0]])
-        count[0] += 1
+
+    def local_copy(src, mid, dst, sem):
+        into = pltpu.make_async_copy(src, mid, into_sem)
         into.start()
-        pending.append((into, out))
-        done.append(out)
+        pending.append((into, pltpu.make_async_copy(mid, dst, sem)))
 
     def flush():
         for into, out in pending:
@@ -220,18 +216,16 @@
             out.start()
         pending.clear()
 
-    fifth = {}
-
     def stage1(j):
         o = CHUNKS[j]
         c = moved(me, "X", o, 1)
         for oo in RING:
             to = moved(me, "y", oo, 1)
-            send(a[0].at[to, :, c], b[0].at[me["y"], :, c], s1.at[0, oo, j], r1.at[0, oo, j], "y", to)
+            send(a[0].at[to, :, c], b[0].at[me["y"], :, c], ssem.at[0, 0], r1.at[0, oo], "y", to)
             to = moved(me, "z", oo, 1)
-            send(a[1].at[to, c], b[1].at[me["z"], c], s1.at[1, oo, j], r1.at[1, oo, j], "z", to)
+            send(a[1].at[to, c], b[1].at[me["z"], c], ssem.at[0, 1], r1.at[1, oo], "z", to)
         if o:
-            send(a[2].at[c], b[2].at[me["X"]], s1.at[2, o, 0], r1.at[2, o, 0], "X", c)
+            send(a[2].at[c], b[2].at[me["X"]], ssem.at[0, 2], r1.at[2, o], "X", c)
 
     for j, o in enumerate(CHUNKS):
         tiles_for(moved(me, "X", o, 1), *a, h_all, x_all, d_all)
@@ -239,22 +233,10 @@
             stage1(j - 1)
     for oo in RING:
         to = moved(me, "y", oo, 1)
-        fifth[oo] = send(v_all.at[to], v_mid.at[me["y"]], vs.at[0, oo], vr.at[0, oo], "y", to)
+        send(v_all.at[to], v_mid.at[me["y"]], v_sem.at[0], v_sem.at[1], "y", to)
     v_mid[me["y"]] = v_all[me["y"]]
     stage1(7)
 
-    def arrived1(g, o):
-        src = moved(me, ORDERS[g][0], o, -1)
-        if g == 2:
-            pltpu.make_async_copy(b[2].at[src], b[2].at[src], r1.at[2, o, 0]).wait()
-            return
-        for j, oc in enumerate(CHUNKS):
-            c = moved(me, "X", oc, 1)
-            ref = b[0].at[src, :, c] if g == 0 else b[1].at[src, c]
-            pltpu.make_async_copy(ref, ref, r1.at[g, o, j]).wait()
-
-    second = {}
-    back2 = {}
     for step in range(8):
         for g, order in enumerate(ORDERS):
             d1, d2, _ = order
@@ -264,34 +246,23 @@
             o1 = offs[step]
             src1 = moved(me, d1, o1, -1)
             if o1:
-                arrived1(g, o1)
+                wait_for(b[g].at[src1], r1.at[g, o1])
             for o2 in offsets(d2):
                 to = moved(me, d2, o2, 1)
                 src = b[g].at[src1, to] if o1 else a[g].at[me[d1], to]
-                second[g, o1, o2] = send(
-                    src, cc[g].at[me[d2], src1], s2.at[g, o1, o2], r2.at[g, o1, o2], d2, to
-                )
+                send(src, cc[g].at[me[d2], src1], ssem.at[1, g], r2.at[g, o2], d2, to)
             flush()
-            done = back2.setdefault(g, [])
+            back = cc[g].at[me[d2], src1]
             if o1:
-                local_copy(b[g].at[src1, me[d2]], bounce2[g].at[o1], cc[g].at[me[d2], src1], done)
+                local_copy(b[g].at[src1, me[d2]], bounce2[g].at[o1], back, out_sem.at[0, g])
             else:
-                out = pltpu.make_async_copy(
-                    a[g].at[me[d1], me[d2]], cc[g].at[me[d2], src1], lsem.at[count[0]]
-                )
-                count[0] += 1
-                out.start()
-                done.append(out)
-    for oo in RING:
-        fifth[oo].wait_recv()
-    v_last = {}
+                pltpu.make_async_copy(a[g].at[me[d1], me[d2]], back, out_sem.at[0, g]).start()
+    wait_for(v_mid.at[0:3], v_sem.at[1])
     for oo in RING:
         to = moved(me, "z", oo, 1)
-        v_last[oo] = send(v_mid.at[:, to], v_out.at[me["z"]], vs.at[1, oo], vr.at[1, oo], "z", to)
+        send(v_mid.at[:, to], v_out.at[me["z"]], v_sem.at[2], v_sem.at[3], "z", to)
     v_out[me["z"]] = v_mid[:, me["z"]]
     flush()
-    third = []
-    last = []
     for step in range(8):
         for g, order in enumerate(ORDERS):
             d1, d2, d3 = order
@@ -300,35 +271,35 @@
                 continue
             o2 = offs[step]
             src2 = moved(me, d2, o2, -1)
-            if o2:
-                for o1 in (0,) + offsets(d1):
-                    second[g, o1, o2].wait_recv()
-            else:
-                for out in back2[g]:
-                    out.wait()
+            wait_for(cc[g].at[src2], r2.at[g, o2] if o2 else out_sem.at[0, g])
             for o3 in offsets(d3):
                 to = moved(me, d3, o3, 1)
-                third.append(
-                    send(
-                        cc[g].at[src2, :, to],
-                        e[g].at[me[d3], src2],
-                        s3.at[g, o2, o3],
-                        r3.at[g, o2, o3],
-                        d3,
-                        to,
-                    )
+                send(
+                    cc[g].at[src2, :, to],
+                    e[g].at[me[d3], src2],
+                    ssem.at[2, g],
+                    r3.at[g],
+                    d3,
+                    to,
                 )
             flush()
-            local_copy(cc[g].at[src2, :, me[d3]], bounce3[g].at[o2], e[g].at[me[d3], src2], last)
+            local_copy(
+                cc[g].at[src2, :, me[d3]],
+                bounce3[g].at[o2],
+                e[g].at[me[d3], src2],
+                out_sem.at[1, g],
+            )
     flush()
-    for oo in RING:
-        v_last[oo].wait_recv()
-    for cp in last:
-        cp.wait()
-    for cp in third:
-        cp.wait_recv()
-    for cp in sends:
-        cp.wait_send()
+    wait_for(v_mid.at[0:3], v_sem.at[3])
+    for g, order in enumerate(ORDERS):
+        n1, n2, n3 = (SIZE[d] for d in order)
+        wait_for(e[g].at[me[order[2]]], out_sem.at[1, g])
+        wait_for(e[g].at[0 : n3 - 1], r3.at[g])
+        wait_for(b[g].at[0 : n1 - 1], ssem.at[0, g])
+        wait_for(cc[g].at[0 : n2 - 1], ssem.at[1, g])
+        wait_for(e[g].at[0 : n3 - 1], ssem.at[2, g])
+    wait_for(v_mid.at[0:3], v_sem.at[0])
+    wait_for(v_mid.at[0:3], v_sem.at[2])
 
 
 def exchange(glob, local, weight, resid, tracks):
@@ -360,15 +331,13 @@
             pltpu.VMEM((24, TRK), f32),
             pltpu.VMEM((16, LOC * TRK), bf16),
             pltpu.VMEM((16, TRK), f32),
-            pltpu.SemaphoreType.DMA((3, 8, 8)),
-            pltpu.SemaphoreType.DMA((3, 8, 8)),
-            pltpu.SemaphoreType.DMA((3, 8, 8)),
-            pltpu.SemaphoreType.DMA((3, 8, 8)),
-            pltpu.SemaphoreType.DMA((3, 8, 8)),
-            pltpu.SemaphoreType.DMA((3, 8, 8)),
-            pltpu.SemaphoreType.DMA((32,)),
-            pltpu.SemaphoreType.DMA((2, 4)),
-            pltpu.SemaphoreType.DMA((2, 4)),
+            pltpu.SemaphoreType.DMA((3, 3)),
+            pltpu.SemaphoreType.DMA((3, 8)),
+            pltpu.SemaphoreType.DMA((3, 8)),
+            pltpu.SemaphoreType.DMA((3,)),
+            pltpu.SemaphoreType.DMA,
+            pltpu.SemaphoreType.DMA((2, 3)),
+            pltpu.SemaphoreType.DMA((4,)),
         ],
         compiler_params=pltpu.CompilerParams(
             collective_id=0, has_side_effects=True, vmem_limit_bytes=60 << 20
@@ -499,65 +468,58 @@
     )(blocks, weak, e0, e1, e2, vec)
 
 
-def finish_kernel(product, diag, part, weak, tile, rhs, got, got_r, ssem, rsem, tsend, trecv):
+def finish_kernel(product, diag, part, weak, tile, rhs, got, got_r, ssem, rsem):
     me = coords()
     row = lax.axis_index("row")
     mine = me["X"]
     owner = row // 2
     barrier, count = greet(me, ("X",))
     pl.semaphore_wait(barrier, count)
-    copies = []
-    for o in WIDE:
-        to = moved(me, "X", o, 1)
-        for i, (src, dst) in enumerate(((product.at[to], got.at[o]), (part, got_r.at[o]))):
-            cp = pltpu.make_async_remote_copy(
-                src_ref=src,
-                dst_ref=dst,
-                send_sem=ssem.at[i, o],
-                recv_sem=rsem.at[i, o],
-                device_id=device(me, "X", to),
-                device_id_type=MESH,
-            )
-            cp.start()
-            copies.append(cp)
-
-    def hand(o):
-        to = moved(me, "X", o, 1)
+
+    def copy(src, dst, i, to):
         return pltpu.make_async_remote_copy(
-            src_ref=diag.at[to],
-            dst_ref=tile,
-            send_sem=tsend.at[o],
-            recv_sem=trecv,
+            src_ref=src,
+            dst_ref=dst,
+            send_sem=ssem.at[i],
+            recv_sem=rsem.at[i],
             device_id=device(me, "X", to),
             device_id_type=MESH,
         )
 
+    def wait_for(ref, sem):
+        pltpu.make_async_copy(ref, ref, sem).wait()
+
+    for o in WIDE:
+        to = moved(me, "X", o, 1)
+        copy(product.at[to], got.at[o - 1], 0, to).start()
+        copy(part, got_r.at[o - 1], 1, to).start()
+
     @pl.when(mine == owner)
     def _():
         for o in WIDE:
-            hand(o).start()
+            to = moved(me, "X", o, 1)
+            copy(diag.at[to], tile, 2, to).start()
         tile[...] = diag[mine]
 
-    for cp in copies:
-        cp.wait_recv()
+    wait_for(got, rsem.at[0])
+    wait_for(got_r, rsem.at[1])
     total = product[mine]
     total_r = part[...]
-    for o in WIDE:
+    for o in range(7):
         total = total + got[o]
         total_r = total_r + got_r[o]
     weak[...] = total
     rhs[...] = total_r
-    for cp in copies:
-        cp.wait_send()
+    wait_for(got, ssem.at[0])
+    wait_for(got_r, ssem.at[1])
 
     @pl.when(mine != owner)
     def _():
-        hand(1).wait_recv()
+        wait_for(tile, rsem.at[2])
 
     @pl.when(mine == owner)
     def _():
-        for o in WIDE:
-            hand(o).wait_send()
+        wait_for(diag.at[0:7], ssem.at[2])
 
 
 def finish(product, diag, part):
@@ -572,12 +534,10 @@
         in_specs=[vmem] * 3,
         out_specs=(vmem,) * 3,
         scratch_shapes=[
-            pltpu.VMEM((8, 64, BW), f32),
-            pltpu.VMEM((8, GB, BW), f32),
-            pltpu.SemaphoreType.DMA((2, 8)),
-            pltpu.SemaphoreType.DMA((2, 8)),
-            pltpu.SemaphoreType.DMA((8,)),
-            pltpu.SemaphoreType.DMA,
+            pltpu.VMEM((7, 64, BW), f32),
+            pltpu.VMEM((7, GB, BW), f32),
+            pltpu.SemaphoreType.DMA((3,)),
+            pltpu.SemaphoreType.DMA((3,)),
         ],
         compiler_params=pltpu.CompilerParams(collective_id=1, has_side_effects=True),
         name="finish",

time: 255 us -> 245 us (0.961)
  Pallas kernels: 249 us -> 238 us
    pallas_call x1, Pallas kernels: 214 us -> 204 us  [exchange(): pl.pallas_call(exchange_kernel, out_shape=tuple(shapes), in_specs=[vmem]...]
where the time goes in v3:
time: 245 us; the launch traced here: 243 us
  Pallas kernels  238 us (97%)
  local copies, waits for them, and re-layouts  2.72 us (1%)
    pallas_call x1, Pallas kernels, exchange(): pl.pallas_call(exchange_kernel, out_shape=tuple(shapes), in_specs=[vmem]...  204 us
    pallas_call x1, Pallas kernels, place(): pl.pallas_call(place_kernel, grid=(8,), in_specs=[pl.BlockSpec(memory_spa...  20.8 us
    pallas_call x1, Pallas kernels, finish(): pl.pallas_call(finish_kernel, out_shape=(jax.ShapeDtypeStruct((64, BW), f...  13.6 us

profile of v3, /device:TPU:17, one launch (start us, length us, event | category | flops | bytes accessed | tf_op | source)
XLA Modules:
  0.0 243.3 jit_solution(860901360441457013)
XLA Ops:
  0.6 203.7 %exchange.1 = (f32[8,4,4,88,128]{4,3,2,1,0:T(8,128)}, f32[4,8,4,88,128]{4,3,2,1,0:T(8,128)}, f32[4,4,8,80,128]{4,3,2,1,0:T(8,128)}, f32[4,4,8,128]{3,2,1,0:T(8,1...) custom-call(bf16[16,256,128]{2,1,0:T(8,128)(2,1)} %bitcast.13, ...), custom_call_target="tpu_custom_call" | custom-call | tf_op jit(solution)/shard_map/exchange/pallas_call | solution.py:317
  204.3 20.8 %place.1 = (f32[1024,2048]{1,0:T(8,128)}, f32[8,64,128]{2,1,0:T(8,128)}, f32[8,128]{1,0:T(8,128)}, f32[8,128,128]{2,1,0:T(8,128)}) custom-call(s32[16,128]{1,0:T(8,128)} %bitcast.20, f32[64,2048]{1,0:T(8,128)} %bitcast.14, f32[8,4,4,88,128]{4,3,2,1,0:T(8,128)} %get-tuple-element.15.e0, f32[4,8,4,88,128]{4,3,2,1,0:T(8,128)} %get-tuple-element.16.e1, ...), custom_call_target="tpu_custom_call" | custom-call | tf_op jit(solution)/shard_map/place/pallas_call | solution.py:435
  225.2 13.6 %finish.1 = (f32[64,128]{1,0:T(8,128)}, f32[128,128]{1,0:T(8,128)}, f32[8,128]{1,0:T(8,128)}) custom-call(f32[8,64,128]{2,1,0:T(8,128)} %get-tuple-element.20.product, f32[8,128,128]{2,1,0:T(8,128)} %get-tuple-element.21.diag, f32[8,128]{1,0:T(8,128)} %get-tuple-element.22.part), custom_call_target="tpu_custom_call" | custom-call | tf_op jit(solution)/shard_map/finish/pallas_call | solution.py:527
  238.8 0.1 broadcast_bitcast_fusion
  238.9 1.8 bitcast_select_fusion
  240.7 1.3 copy.13
  242.0 1.4 copy.14
  (1 shorter events, 0.0 us)

commit v4 on v3

--- a/solution.py
+++ b/solution.py
@@ -18,6 +18,8 @@
 ORDERS = (("y", "z", "X"), ("z", "X", "y"), ("X", "y", "z"))
 RING = (1, 3, 2)
 WIDE = (2, 6, 3, 7, 4, 5, 1)
+UNROLL1 = 2
+UNROLL2 = 2
 CHUNKS = (2, 6, 3, 7, 0, 4, 5, 1)
 MESH = pl.DeviceIdType.MESH
 f32 = jnp.float32
@@ -40,13 +42,11 @@
     return lax.dot_general(a, b, (((1,), (0,)), ((), ())), preferred_element_type=f32)
 
 
-def local_terms(glob, local, weight, resid, tracks, h_all, x_all, d_all, v_all, sums, q_ref, k_ref):
+def local_terms(glob, local, weight, resid, tracks, h_all, x_all, sums, q_ref, k_ref):
     sums[...] = jnp.zeros_like(sums)
 
     def first(s, carry):
-        g = glob[s]
-        gt = jnp.transpose(g.astype(f32))
-        gt_low = gt.astype(bf16)
+        gt_low = jnp.transpose(glob[s].astype(f32)).astype(bf16)
         t = tracks[pl.ds(s, 1), :]
         w = weight[pl.ds(s, 1), :]
         r = resid[pl.ds(s, 1), :]
@@ -67,12 +67,9 @@
         hot_low = jnp.where(hot, jnp.ones((), f32), zero).astype(bf16)
         hi, mid, low = split3(stacked)
         sums[...] += nt(hi, hot_low) + nt(mid, hot_low) + nt(low, hot_low)
-        d_all[row, :] = nn((gt * w).astype(bf16), g)
-        wr = jnp.broadcast_to((w * r).astype(bf16), (16, PER))
-        v_all[s // 4, s % 4] = nn(wr, g)[:8]
         return carry
 
-    lax.fori_loop(0, LAYERS, first, 0)
+    lax.fori_loop(0, LAYERS, first, 0, unroll=UNROLL1)
 
     one = jnp.ones((1, TRK), f32)
     nil = jnp.zeros((1, TRK), f32)
@@ -108,13 +105,23 @@
             for l in range(1, LOC):
                 x = x + h[l] * k_ref[4 * l + j : 4 * l + j + 1, :]
             x_all[row, j * TRK : (j + 1) * TRK] = (-x).astype(bf16)
-        v_all[s // 4, s % 4] = v_all[s // 4, s % 4] + nt(q_ref[...], x_all[row, :])[:8]
         return carry
 
-    lax.fori_loop(0, LAYERS, second, 0)
-
-
-def tiles_for(c, a0, a1, a2, h_all, x_all, d_all):
+    lax.fori_loop(0, LAYERS, second, 0, unroll=UNROLL2)
+
+
+def vectors(glob, weight, resid, x_all, q_ref, v_all):
+    def term(s, carry):
+        wr = (weight[pl.ds(s, 1), :] * resid[pl.ds(s, 1), :]).astype(bf16)
+        x = x_all[pl.ds(pl.multiple_of(s * BW, BW), BW), :]
+        both = nn(jnp.broadcast_to(wr, (16, PER)), glob[s]) + nt(q_ref[...], x)
+        v_all[s // 4, s % 4] = both[:8]
+        return carry
+
+    lax.fori_loop(0, LAYERS, term, 0)
+
+
+def tiles_for(c, start, stop, a0, a1, a2, h_all, x_all):
     right = h_all[pl.ds(pl.multiple_of(c * 2 * BW, 2 * BW), 2 * BW), :]
 
     def gram(y, carry):
@@ -127,15 +134,22 @@
             a2[c, y, z] = part[48:BW, BW:]
         return carry
 
-    lax.fori_loop(0, 4, gram, 0)
+    lax.fori_loop(start, stop, gram, 0)
+
+
+def diagonal(c, glob, weight, a0, a1, a2):
+    def own(s):
+        g = glob[s]
+        return nn((jnp.transpose(g.astype(f32)) * weight[pl.ds(s, 1), :]).astype(bf16), g)
+
     s = 2 * c
     y, z = s // 4, s % 4
-    base = pl.multiple_of(s * BW, BW)
-    a0[y, z, c] += d_all[pl.ds(base, 88), :]
-    a1[z, c, y, 0:40] += d_all[pl.ds(base + 88, 40), :]
-    base = pl.multiple_of(s * BW + BW, BW)
-    a1[z + 1, c, y, 40:88] += d_all[pl.ds(base, 48), :]
-    a2[c, y, z + 1] += d_all[pl.ds(base + 48, 80), :]
+    d = own(s)
+    a0[y, z, c] += d[0:88]
+    a1[z, c, y, 0:40] += d[88:BW]
+    d = own(s + 1)
+    a1[z + 1, c, y, 40:88] += d[0:48]
+    a2[c, y, z + 1] += d[48:BW]
 
 
 def coords():
@@ -180,13 +194,11 @@
     e, v_out, b, cc = refs[0:3], refs[3], refs[4:7], refs[7:10]
     a = refs[10:13]
     bounce2, bounce3 = refs[13:16], refs[16:19]
-    h_all, x_all, d_all, v_all, v_mid, sums, q_ref, k_ref = refs[19:27]
-    ssem, r1, r2, r3, into_sem, out_sem, v_sem = refs[27:34]
+    h_all, x_all, v_all, v_mid, sums, q_ref, k_ref = refs[19:26]
+    ssem, r1, r2, r3, into_sem, out_sem, v_sem = refs[26:33]
     me = coords()
     barrier, count = greet(me, ("y", "z", "X"))
-    local_terms(
-        glob, local, weight, resid, tracks, h_all, x_all, d_all, v_all, sums, q_ref, k_ref
-    )
+    local_terms(glob, local, weight, resid, tracks, h_all, x_all, sums, q_ref, k_ref)
     pl.semaphore_wait(barrier, count)
 
     def send(src, dst, ssem, rsem, dim, place):
@@ -228,14 +240,18 @@
             send(a[2].at[c], b[2].at[me["X"]], ssem.at[0, 2], r1.at[2, o], "X", c)
 
     for j, o in enumerate(CHUNKS):
-        tiles_for(moved(me, "X", o, 1), *a, h_all, x_all, d_all)
+        c = moved(me, "X", o, 1)
+        tiles_for(c, 0, 1, *a, h_all, x_all)
         if j:
             stage1(j - 1)
+        tiles_for(c, 1, 4, *a, h_all, x_all)
+        diagonal(c, glob, weight, *a)
+    vectors(glob, weight, resid, x_all, q_ref, v_all)
+    stage1(7)
     for oo in RING:
         to = moved(me, "y", oo, 1)
         send(v_all.at[to], v_mid.at[me["y"]], v_sem.at[0], v_sem.at[1], "y", to)
     v_mid[me["y"]] = v_all[me["y"]]
-    stage1(7)
 
     for step in range(8):
         for g, order in enumerate(ORDERS):
@@ -325,7 +341,6 @@
         + [
             pltpu.VMEM((LAYERS * BW, LOC * TRK), bf16),
             pltpu.VMEM((LAYERS * BW, LOC * TRK), bf16),
-            pltpu.VMEM((LAYERS * BW, BW), f32),
             pltpu.VMEM((4, 4, 8, BW), f32),
             pltpu.VMEM((4, 4, 8, BW), f32),
             pltpu.VMEM((24, TRK), f32),
@@ -347,108 +362,99 @@
     return out[:4]
 
 
-def place_kernel(blocks, weak, e0, e1, e2, vec, schur, product, rhs, diag, acc, w_ref, p_ref, sem):
-    xb = pl.program_id(0)
+def place_kernel(
+    blocks, weak, e0, e1, e2, vec, schur, product, rhs, diag, b0, b1, b2, acc, w_ref, p_ref, isem, sem
+):
     row, col = lax.axis_index("row"), lax.axis_index("col")
 
-    @pl.when(xb == 0)
-    def _():
-        acc[...] = jnp.zeros_like(acc)
-        rhs[...] = jnp.zeros_like(rhs)
-
-        def term(i, carry):
-            k = blocks[row, i * 8 + col]
-            rhs[pl.ds(k, 1), :] += vec[i % 4, i // 4, 0:1]
+    def fetch(i):
+        return (
+            pltpu.make_async_copy(e0.at[i], b0.at[i], isem.at[0, i]),
+            pltpu.make_async_copy(e1.at[:, i], b1.at[:, i], isem.at[1, i]),
+            pltpu.make_async_copy(e2.at[:, :, i], b2.at[:, :, i], isem.at[2, i]),
+        )
+
+    for i in range(8):
+        for cp in fetch(i):
+            cp.start()
+    acc[...] = jnp.zeros_like(acc)
+    rhs[...] = jnp.zeros_like(rhs)
+    w = weak[...]
+    w_hi = w.astype(bf16)
+    w_ref[0:64, :] = w_hi
+    w_ref[64:128, :] = (w - w_hi.astype(f32)).astype(bf16)
+    p_ref[...] = jnp.zeros_like(p_ref)
+
+    def term(i, carry):
+        k = blocks[row, i * 8 + col]
+        rhs[pl.ds(k, 1), :] += vec[i % 4, i // 4, 0:1]
+        return carry
+
+    lax.fori_loop(0, 16, term, 0)
+
+    def batch(xb, carry):
+        for cp in fetch(xb):
+            cp.wait()
+
+        def bundle(i, carry):
+            y, z = i // 4, i % 4
+            b = i * 8 + xb
+            l0 = pl.multiple_of(blocks[2 * col, b] * BW, BW)
+            l1 = pl.multiple_of(blocks[2 * col + 1, b] * BW + GB * BW, BW)
+            r = pl.multiple_of(blocks[row, b] * BW, BW)
+            acc[pl.ds(r, 88), pl.ds(l0, BW)] += b0[xb, z, y]
+            acc[pl.ds(r + 88, 40), pl.ds(l0, BW)] += b1[y, xb, z, 0:40]
+            acc[pl.ds(r, 48), pl.ds(l1, BW)] += b1[y, xb, z, 40:88]
+            acc[pl.ds(r + 48, 80), pl.ds(l1, BW)] += b2[z, y, xb]
             return carry
 
-        lax.fori_loop(0, 16, term, 0)
-
-    def bundle(i, carry):
-        y, z = i // 4, i % 4
-        b = i * 8 + xb
-        l0 = pl.multiple_of(blocks[2 * col, b] * BW, BW)
-        l1 = pl.multiple_of(blocks[2 * col + 1, b] * BW + GB * BW, BW)
-        r = pl.multiple_of(blocks[row, b] * BW, BW)
-        acc[pl.ds(r, 88), pl.ds(l0, BW)] += e0[0, z, y]
-        acc[pl.ds(r + 88, 40), pl.ds(l0, BW)] += e1[y, 0, z, 0:40]
-        acc[pl.ds(r, 48), pl.ds(l1, BW)] += e1[y, 0, z, 40:88]
-        acc[pl.ds(r + 48, 80), pl.ds(l1, BW)] += e2[z, y, 0]
+        return lax.fori_loop(0, 16, bundle, carry)
+
+    lax.fori_loop(0, 8, batch, 0)
+
+    def copy_out(ch):
+        cols = pl.ds(pl.multiple_of(ch * 256, 256), 256)
+        return pltpu.make_async_copy(acc.at[:, cols], schur.at[:, cols], sem.at[ch])
+
+    def chunk(ch, carry):
+        cols = pl.ds(pl.multiple_of(ch * 256, 256), 256)
+        wc = w_ref[:, cols]
+        v = acc[:, cols]
+        hi = v.astype(bf16)
+        lo = (v - hi.astype(f32)).astype(bf16)
+        p_ref[...] += nt(hi, wc) + nt(lo, wc)
+
+        @pl.when(ch // 4 == row % 2)
+        def _():
+            for m in range(2):
+                k = 2 * (ch % 4) + m
+                diag[k] = acc[
+                    pl.ds(pl.multiple_of(k * BW, BW), BW),
+                    pl.ds(pl.multiple_of(ch * 256 + m * BW, BW), BW),
+                ]
+
+            @pl.when(col == row // 2)
+            def _():
+                acc[:, cols] = jnp.zeros((GB * BW, 256), f32)
+
+        copy_out(ch).start()
         return carry
 
-    lax.fori_loop(0, 16, bundle, 0)
-
-    @pl.when(xb == 7)
-    def _():
-        w = weak[...]
-        w_hi = w.astype(bf16)
-        w_ref[0:64, :] = w_hi
-        w_ref[64:128, :] = (w - w_hi.astype(f32)).astype(bf16)
-        p_ref[...] = jnp.zeros_like(p_ref)
-
-        def copy_out(ch):
-            cols = pl.ds(pl.multiple_of(ch * 256, 256), 256)
-            return pltpu.make_async_copy(acc.at[:, cols], schur.at[:, cols], sem.at[ch])
-
-        def chunk(ch, carry):
-            cols = pl.ds(pl.multiple_of(ch * 256, 256), 256)
-            wc = w_ref[:, cols]
-
-            def multiply(i, carry):
-                r = pl.ds(pl.multiple_of(i * 256, 256), 256)
-                v = acc[r, cols]
-                hi = v.astype(bf16)
-                lo = (v - hi.astype(f32)).astype(bf16)
-                p_ref[r, :] += nt(hi, wc) + nt(lo, wc)
-                return carry
-
-            lax.fori_loop(0, 4, multiply, 0)
-
-            @pl.when(ch // 4 == row % 2)
-            def _():
-                for m in range(2):
-                    k = 2 * (ch % 4) + m
-                    diag[k] = acc[
-                        pl.ds(pl.multiple_of(k * BW, BW), BW),
-                        pl.ds(pl.multiple_of(ch * 256 + m * BW, BW), BW),
-                    ]
-
-                @pl.when(col == row // 2)
-                def _():
-                    acc[:, cols] = jnp.zeros((GB * BW, 256), f32)
-
-            copy_out(ch).start()
-            return carry
-
-        lax.fori_loop(0, 8, chunk, 0)
-        for k in range(GB):
-            pt = jnp.transpose(p_ref[k * BW : (k + 1) * BW, :])
-            product[k] = pt[0:64] + pt[64:128]
-        for ch in range(8):
-            copy_out(ch).wait()
+    lax.fori_loop(0, 8, chunk, 0)
+    for k in range(GB):
+        pt = jnp.transpose(p_ref[k * BW : (k + 1) * BW, :])
+        product[k] = pt[0:64] + pt[64:128]
+    for ch in range(8):
+        copy_out(ch).wait()
 
 
 def place(blocks, weak, e0, e1, e2, vec):
-    def whole(*shape):
-        return pl.BlockSpec(shape, lambda i: (0,) * len(shape))
-
-    r0, r1, r2 = ROWS
+    vmem = pl.BlockSpec(memory_space=pltpu.VMEM)
+    any_ = pl.BlockSpec(memory_space=pl.ANY)
     return pl.pallas_call(
         place_kernel,
-        grid=(8,),
-        in_specs=[
-            pl.BlockSpec(memory_space=pltpu.SMEM),
-            whole(64, 2 * GB * BW),
-            pl.BlockSpec((1, 4, 4, r0, BW), lambda i: (i, 0, 0, 0, 0)),
-            pl.BlockSpec((4, 1, 4, r1, BW), lambda i: (0, i, 0, 0, 0)),
-            pl.BlockSpec((4, 4, 1, r2, BW), lambda i: (0, 0, i, 0, 0)),
-            whole(4, 4, 8, BW),
-        ],
-        out_specs=(
-            pl.BlockSpec(memory_space=pl.ANY),
-            whole(GB, 64, BW),
-            whole(GB, BW),
-            whole(GB, BW, BW),
-        ),
+        in_specs=[pl.BlockSpec(memory_space=pltpu.SMEM), vmem, any_, any_, any_, vmem],
+        out_specs=(any_, vmem, vmem, vmem),
         out_shape=(
             jax.ShapeDtypeStruct((GB * BW, 2 * GB * BW), f32),
             jax.ShapeDtypeStruct((GB, 64, BW), f32),
@@ -456,14 +462,16 @@
             jax.ShapeDtypeStruct((GB, BW, BW), f32),
         ),
         scratch_shapes=[
+            pltpu.VMEM(e0.shape, f32),
+            pltpu.VMEM(e1.shape, f32),
+            pltpu.VMEM(e2.shape, f32),
             pltpu.VMEM((GB * BW, 2 * GB * BW), f32),
             pltpu.VMEM((BW, 2 * GB * BW), bf16),
             pltpu.VMEM((GB * BW, BW), f32),
+            pltpu.SemaphoreType.DMA((3, 8)),
             pltpu.SemaphoreType.DMA((8,)),
         ],
-        compiler_params=pltpu.CompilerParams(
-            dimension_semantics=("arbitrary",), vmem_limit_bytes=56 << 20
-        ),
+        compiler_params=pltpu.CompilerParams(vmem_limit_bytes=56 << 20),
         name="place",
     )(blocks, weak, e0, e1, e2, vec)
 
@@ -544,12 +552,33 @@
     )(product, diag, part)
 
 
+def emit_kernel(weak_in, tile, rhs_in, weak, layer, rhs):
+    col = lax.axis_index("col")
+    weak[...] = weak_in[...]
+    rhs[...] = rhs_in[...]
+    layer[...] = jnp.zeros_like(layer)
+    layer[pl.ds(pl.multiple_of(col * BW, BW), BW), :] = tile[...]
+
+
+def emit(weak, tile, rhs):
+    vmem = pl.BlockSpec(memory_space=pltpu.VMEM)
+    return pl.pallas_call(
+        emit_kernel,
+        out_shape=(
+            jax.ShapeDtypeStruct((64, BW), f32),
+            jax.ShapeDtypeStruct((GB * BW, BW), f32),
+            jax.ShapeDtypeStruct((GB, BW), f32),
+        ),
+        in_specs=[vmem] * 3,
+        out_specs=(vmem,) * 3,
+        name="emit",
+    )(weak, tile, rhs)
+
+
 def body(glob_derivs, local_derivs, weights, residuals, track_ids, module_blocks, weak_modes):
     e = exchange(glob_derivs[0], local_derivs[0], weights[0], residuals[0], track_ids[0])
     schur, product, part, diag = place(module_blocks.T, weak_modes.T, *e)
-    weak, tile, rhs = finish(product, diag, part)
-    here = jnp.arange(GB)[:, None, None] == lax.axis_index("col")
-    layer = jnp.where(here, tile[None], jnp.zeros((), f32)).reshape(GB * BW, BW)
+    weak, layer, rhs = emit(*finish(product, diag, part))
     return schur, layer, rhs.reshape(GB * BW), weak.T
 
 

time: 245 us -> 229 us (0.935)
  Pallas kernels: 238 us -> 228 us
  local copies, waits for them, and re-layouts: 2.72 us -> 0 us
    pallas_call x1 -> x2, Pallas kernels: 20.8 us -> 15.5 us  [the longest x1 13.8 us: place(): pl.pallas_call(place_kernel, in_specs=[pl.BlockSpec(memory_space=pltpu.SM...]
    pallas_call x1, Pallas kernels: 204 us -> 199 us  [exchange(): pl.pallas_call(exchange_kernel, out_shape=tuple(shapes), in_specs=[vmem]...]
    unnamed x2 -> x0, local copies, waits for them, and re-layouts: 2.65 us -> none
where the time goes in v4:
time: 229 us; the launch traced here: 228 us
  Pallas kernels  228 us (100%)
    pallas_call x1, Pallas kernels, exchange(): pl.pallas_call(exchange_kernel, out_shape=tuple(shapes), in_specs=[vmem]...  199 us
    pallas_call x1, Pallas kernels, place(): pl.pallas_call(place_kernel, in_specs=[pl.BlockSpec(memory_space=pltpu.SM...  13.8 us
    pallas_call x1, Pallas kernels, finish(): pl.pallas_call(finish_kernel, out_shape=(jax.ShapeDtypeStruct((64, BW), f...  13.6 us

profile of v4, /device:TPU:17, one launch (start us, length us, event | category | flops | bytes accessed | tf_op | source)
XLA Modules:
  0.0 228.4 jit_solution(7488074223148854734)
XLA Ops:
  0.6 198.7 %exchange.1 = (f32[8,4,4,88,128]{4,3,2,1,0:T(8,128)}, f32[4,8,4,88,128]{4,3,2,1,0:T(8,128)}, f32[4,4,8,80,128]{4,3,2,1,0:T(8,128)}, f32[4,4,8,128]{3,2,1,0:T(8,1...) custom-call(bf16[16,256,128]{2,1,0:T(8,128)(2,1)} %bitcast.9, ...), custom_call_target="tpu_custom_call" | custom-call | tf_op jit(solution)/shard_map/exchange/pallas_call | solution.py:333
  199.3 13.8 %place.1 = (f32[1024,2048]{1,0:T(8,128)}, f32[8,64,128]{2,1,0:T(8,128)}, f32[8,128]{1,0:T(8,128)}, f32[8,128,128]{2,1,0:T(8,128)}) custom-call(s32[16,128]{1,0:T(8,128)} %bitcast.15, f32[64,2048]{1,0:T(8,128)} %bitcast.10, f32[8,4,4,88,128]{4,3,2,1,0:T(8,128)} %get-tuple-element.18.e0, f32[4,8,4,88,128]{4,3,2,1,0:T(8,128)} %get-tuple-element.19.e1, ...), custom_call_target="tpu_custom_call" | custom-call | tf_op jit(solution)/shard_map/place/pallas_call | solution.py:454
  213.1 13.6 %finish.1 = (f32[64,128]{1,0:T(8,128)}, f32[128,128]{1,0:T(8,128)}, f32[8,128]{1,0:T(8,128)}) custom-call(f32[8,64,128]{2,1,0:T(8,128)} %get-tuple-element.23.product, f32[8,128,128]{2,1,0:T(8,128)} %get-tuple-element.24.diag, f32[8,128]{1,0:T(8,128)} %get-tuple-element.25.part), custom_call_target="tpu_custom_call" | custom-call | tf_op jit(solution)/shard_map/finish/pallas_call | solution.py:535
  226.7 1.7 emit.1

commit v5 on v4

--- a/solution.py
+++ b/solution.py
@@ -190,14 +190,24 @@
     return barrier, count
 
 
-def exchange_kernel(glob, local, weight, resid, tracks, *refs):
+def exchange_kernel(*refs):
+    given, refs = refs[:5], refs[5:]
     e, v_out, b, cc = refs[0:3], refs[3], refs[4:7], refs[7:10]
     a = refs[10:13]
-    bounce2, bounce3 = refs[13:16], refs[16:19]
-    h_all, x_all, v_all, v_mid, sums, q_ref, k_ref = refs[19:26]
-    ssem, r1, r2, r3, into_sem, out_sem, v_sem = refs[26:33]
+    bounce2 = refs[13:16]
+    h_all, x_all, v_all, v_mid, sums, q_ref, k_ref = refs[16:23]
+    ssem, r1, r2, r3, into_sem, out_sem, v_sem = refs[23:30]
+    glob, local, weight, resid, tracks, in_sem = refs[30:36]
+    loads = [
+        pltpu.make_async_copy(src, dst, in_sem.at[i])
+        for i, (src, dst) in enumerate(zip(given, (glob, local, weight, resid, tracks)))
+    ]
+    for cp in loads:
+        cp.start()
     me = coords()
     barrier, count = greet(me, ("y", "z", "X"))
+    for cp in loads:
+        cp.wait()
     local_terms(glob, local, weight, resid, tracks, h_all, x_all, sums, q_ref, k_ref)
     pl.semaphore_wait(barrier, count)
 
@@ -298,14 +308,9 @@
                     d3,
                     to,
                 )
-            flush()
-            local_copy(
-                cc[g].at[src2, :, me[d3]],
-                bounce3[g].at[o2],
-                e[g].at[me[d3], src2],
-                out_sem.at[1, g],
-            )
-    flush()
+            pltpu.make_async_copy(
+                cc[g].at[src2, :, me[d3]], e[g].at[me[d3], src2], out_sem.at[1, g]
+            ).start()
     wait_for(v_mid.at[0:3], v_sem.at[3])
     for g, order in enumerate(ORDERS):
         n1, n2, n3 = (SIZE[d] for d in order)
@@ -323,7 +328,7 @@
     items = [(rows, BW) for rows in ROWS]
     both = list(zip(sizes, items))
     shapes = (
-        [jax.ShapeDtypeStruct((n3, n2, n1) + it, f32) for (n1, n2, n3), it in both]
+        [pltpu.VMEM((n3, n2, n1) + it, f32) for (n1, n2, n3), it in both]
         + [jax.ShapeDtypeStruct((4, 4, 8, BW), f32)]
         + [jax.ShapeDtypeStruct((n1, n2, n3) + it, f32) for (n1, n2, n3), it in both]
         + [jax.ShapeDtypeStruct((n2, n1, n3) + it, f32) for (n1, n2, n3), it in both]
@@ -333,11 +338,10 @@
     out = pl.pallas_call(
         exchange_kernel,
         out_shape=tuple(shapes),
-        in_specs=[vmem] * 5,
-        out_specs=(any_,) * 3 + (vmem,) + (any_,) * 6,
+        in_specs=[pl.BlockSpec(memory_space=pltpu.HBM)] * 5,
+        out_specs=(vmem,) * 3 + (vmem,) + (any_,) * 6,
         scratch_shapes=[pltpu.VMEM(n + it, f32) for n, it in both]
         + [pltpu.VMEM((n1, n3) + it, f32) for (n1, n2, n3), it in both]
-        + [pltpu.VMEM((n2, n1) + it, f32) for (n1, n2, n3), it in both]
         + [
             pltpu.VMEM((LAYERS * BW, LOC * TRK), bf16),
             pltpu.VMEM((LAYERS * BW, LOC * TRK), bf16),
@@ -353,9 +357,15 @@
             pltpu.SemaphoreType.DMA,
             pltpu.SemaphoreType.DMA((2, 3)),
             pltpu.SemaphoreType.DMA((4,)),
+            pltpu.VMEM(glob.shape, bf16),
+            pltpu.VMEM(local.shape, f32),
+            pltpu.VMEM(weight.shape, f32),
+            pltpu.VMEM(resid.shape, f32),
+            pltpu.VMEM(tracks.shape, jnp.int32),
+            pltpu.SemaphoreType.DMA((5,)),
         ],
         compiler_params=pltpu.CompilerParams(
-            collective_id=0, has_side_effects=True, vmem_limit_bytes=60 << 20
+            collective_id=0, has_side_effects=True, vmem_limit_bytes=36 << 20
         ),
         name="exchange",
     )(glob, local, weight, resid, tracks)
@@ -363,22 +373,18 @@
 
 
 def place_kernel(
-    blocks, weak, e0, e1, e2, vec, schur, product, rhs, diag, b0, b1, b2, acc, w_ref, p_ref, isem, sem
+    given_b, given_w, e0, e1, e2, vec, schur, product, rhs, diag, acc, w_ref, p_ref, blocks, weak, sem, lsem
 ):
     row, col = lax.axis_index("row"), lax.axis_index("col")
 
-    def fetch(i):
-        return (
-            pltpu.make_async_copy(e0.at[i], b0.at[i], isem.at[0, i]),
-            pltpu.make_async_copy(e1.at[:, i], b1.at[:, i], isem.at[1, i]),
-            pltpu.make_async_copy(e2.at[:, :, i], b2.at[:, :, i], isem.at[2, i]),
-        )
-
-    for i in range(8):
-        for cp in fetch(i):
-            cp.start()
+    load_b = pltpu.make_async_copy(given_b, blocks, lsem.at[0])
+    load_w = pltpu.make_async_copy(given_w, weak, lsem.at[1])
+    load_b.start()
+    load_w.start()
     acc[...] = jnp.zeros_like(acc)
     rhs[...] = jnp.zeros_like(rhs)
+    load_w.wait()
+    load_b.wait()
     w = weak[...]
     w_hi = w.astype(bf16)
     w_ref[0:64, :] = w_hi
@@ -393,19 +399,16 @@
     lax.fori_loop(0, 16, term, 0)
 
     def batch(xb, carry):
-        for cp in fetch(xb):
-            cp.wait()
-
         def bundle(i, carry):
             y, z = i // 4, i % 4
             b = i * 8 + xb
             l0 = pl.multiple_of(blocks[2 * col, b] * BW, BW)
             l1 = pl.multiple_of(blocks[2 * col + 1, b] * BW + GB * BW, BW)
             r = pl.multiple_of(blocks[row, b] * BW, BW)
-            acc[pl.ds(r, 88), pl.ds(l0, BW)] += b0[xb, z, y]
-            acc[pl.ds(r + 88, 40), pl.ds(l0, BW)] += b1[y, xb, z, 0:40]
-            acc[pl.ds(r, 48), pl.ds(l1, BW)] += b1[y, xb, z, 40:88]
-            acc[pl.ds(r + 48, 80), pl.ds(l1, BW)] += b2[z, y, xb]
+            acc[pl.ds(r, 88), pl.ds(l0, BW)] += e0[xb, z, y]
+            acc[pl.ds(r + 88, 40), pl.ds(l0, BW)] += e1[y, xb, z, 0:40]
+            acc[pl.ds(r, 48), pl.ds(l1, BW)] += e1[y, xb, z, 40:88]
+            acc[pl.ds(r + 48, 80), pl.ds(l1, BW)] += e2[z, y, xb]
             return carry
 
         return lax.fori_loop(0, 16, bundle, carry)
@@ -451,9 +454,10 @@
 def place(blocks, weak, e0, e1, e2, vec):
     vmem = pl.BlockSpec(memory_space=pltpu.VMEM)
     any_ = pl.BlockSpec(memory_space=pl.ANY)
+    hbm = pl.BlockSpec(memory_space=pltpu.HBM)
     return pl.pallas_call(
         place_kernel,
-        in_specs=[pl.BlockSpec(memory_space=pltpu.SMEM), vmem, any_, any_, any_, vmem],
+        in_specs=[hbm, hbm, vmem, vmem, vmem, vmem],
         out_specs=(any_, vmem, vmem, vmem),
         out_shape=(
             jax.ShapeDtypeStruct((GB * BW, 2 * GB * BW), f32),
@@ -462,16 +466,15 @@
             jax.ShapeDtypeStruct((GB, BW, BW), f32),
         ),
         scratch_shapes=[
-            pltpu.VMEM(e0.shape, f32),
-            pltpu.VMEM(e1.shape, f32),
-            pltpu.VMEM(e2.shape, f32),
             pltpu.VMEM((GB * BW, 2 * GB * BW), f32),
             pltpu.VMEM((BW, 2 * GB * BW), bf16),
             pltpu.VMEM((GB * BW, BW), f32),
-            pltpu.SemaphoreType.DMA((3, 8)),
+            pltpu.SMEM(blocks.shape, jnp.int32),
+            pltpu.VMEM(weak.shape, f32),
             pltpu.SemaphoreType.DMA((8,)),
+            pltpu.SemaphoreType.DMA((2,)),
         ],
-        compiler_params=pltpu.CompilerParams(vmem_limit_bytes=56 << 20),
+        compiler_params=pltpu.CompilerParams(vmem_limit_bytes=20 << 20),
         name="place",
     )(blocks, weak, e0, e1, e2, vec)
 
@@ -547,7 +550,9 @@
             pltpu.SemaphoreType.DMA((3,)),
             pltpu.SemaphoreType.DMA((3,)),
         ],
-        compiler_params=pltpu.CompilerParams(collective_id=1, has_side_effects=True),
+        compiler_params=pltpu.CompilerParams(
+            collective_id=1, has_side_effects=True, vmem_limit_bytes=8 << 20
+        ),
         name="finish",
     )(product, diag, part)
 
@@ -571,13 +576,18 @@
         ),
         in_specs=[vmem] * 3,
         out_specs=(vmem,) * 3,
+        compiler_params=pltpu.CompilerParams(vmem_limit_bytes=8 << 20),
         name="emit",
     )(weak, tile, rhs)
 
 
 def body(glob_derivs, local_derivs, weights, residuals, track_ids, module_blocks, weak_modes):
-    e = exchange(glob_derivs[0], local_derivs[0], weights[0], residuals[0], track_ids[0])
-    schur, product, part, diag = place(module_blocks.T, weak_modes.T, *e)
+    def stay(v):
+        return pltpu.with_memory_space_constraint(v, pltpu.HBM)
+
+    inputs = (glob_derivs, local_derivs, weights, residuals, track_ids)
+    e = exchange(*[stay(v[0]) for v in inputs])
+    schur, product, part, diag = place(stay(module_blocks.T), stay(weak_modes.T), *e)
     weak, layer, rhs = emit(*finish(product, diag, part))
     return schur, layer, rhs.reshape(GB * BW), weak.T
 

time: 229 us -> 224 us (0.978)
  Pallas kernels: 228 us -> 222 us
    pallas_call x2, Pallas kernels: 212 us -> 210 us  [the longest x1 198 us: exchange(): pl.pallas_call(exchange_kernel, out_shape=tuple(shapes), in_specs=[pl.Blo...]
where the time goes in v5:
time: 224 us; the launch traced here: 223 us
  Pallas kernels  222 us (99%)
    pallas_call x1, Pallas kernels, exchange(): pl.pallas_call(exchange_kernel, out_shape=tuple(shapes), in_specs=[pl.Blo...  198 us
    pallas_call x1, Pallas kernels, finish(): pl.pallas_call(finish_kernel, out_shape=(jax.ShapeDtypeStruct((64, BW), f...  11.9 us
    pallas_call x1, Pallas kernels, place(): pl.pallas_call(place_kernel, in_specs=[hbm, hbm, vmem, vmem, vmem, vmem],...  11.7 us

profile of v5, /device:TPU:17, one launch (start us, length us, event | category | flops | bytes accessed | tf_op | source)
XLA Modules:
  0.0 223.0 jit_solution(11791571533943965292)
XLA Ops:
  0.6 197.9 %exchange.1 = (f32[8,4,4,88,128]{4,3,2,1,0:T(8,128)S(1)}, f32[4,8,4,88,128]{4,3,2,1,0:T(8,128)S(1)}, f32[4,4,8,80,128]{4,3,2,1,0:T(8,128)S(1)}, f32[4,4,8,128]{3...) custom-call(bf16[16,256,128]{2,1,0:T(8,128)(2,1)} %bitcast.9, ...), custom_call_target="tpu_custom_call" | custom-call | tf_op jit(solution)/shard_map/exchange/pallas_call | solution.py:338
  198.6 11.7 %place.1 = (f32[1024,2048]{1,0:T(8,128)}, f32[8,64,128]{2,1,0:T(8,128)S(1)}, f32[8,128]{1,0:T(8,128)S(1)}, f32[8,128,128]{2,1,0:T(8,128)S(1)}) custom-call(s32[16,128]{1,0:T(8,128)} %bitcast.15, f32[64,2048]{1,0:T(8,128)} %bitcast.10, f32[8,4,4,88,128]{4,3,2,1,0:T(8,128)S(1)} %get-tuple-element.18.e0, f32[4,8,4,88,128]{4,3,2,1,0:T(8,128)S(1)} %get-tuple-element.19.e1, ...), custom_call_target="tpu_custom_call" | custom-call | tf_op jit(solution)/shard_map/place/pallas_call | solution.py:458
  210.3 11.9 %finish.1 = (f32[64,128]{1,0:T(8,128)S(1)}, f32[128,128]{1,0:T(8,128)S(1)}, f32[8,128]{1,0:T(8,128)S(1)}) custom-call(f32[8,64,128]{2,1,0:T(8,128)S(1)} %get-tuple-element.23.product, f32[8,128,128]{2,1,0:T(8,128)S(1)} %get-tuple-element.24.diag, f32[8,128]{1,0:T(8,128)S(1)} %get-tuple-element.25.part), custom_call_target="tpu_custom_call" | custom-call | tf_op jit(solution)/shard_map/finish/pallas_call | solution.py:538
  222.2 0.8 emit.1

commit v6 on v5

--- a/solution.py
+++ b/solution.py
@@ -18,8 +18,8 @@
 ORDERS = (("y", "z", "X"), ("z", "X", "y"), ("X", "y", "z"))
 RING = (1, 3, 2)
 WIDE = (2, 6, 3, 7, 4, 5, 1)
-UNROLL1 = 2
-UNROLL2 = 2
+UNROLL1 = 4
+UNROLL2 = 4
 CHUNKS = (2, 6, 3, 7, 0, 4, 5, 1)
 MESH = pl.DeviceIdType.MESH
 f32 = jnp.float32
@@ -373,7 +373,7 @@
 
 
 def place_kernel(
-    given_b, given_w, e0, e1, e2, vec, schur, product, rhs, diag, acc, w_ref, p_ref, blocks, weak, sem, lsem
+    given_b, given_w, e0, e1, e2, vec, schur, product, diag, acc0, acc1, w_ref, p_ref, blocks, weak, rhs, sem, lsem
 ):
     row, col = lax.axis_index("row"), lax.axis_index("col")
 
@@ -381,7 +381,8 @@
     load_w = pltpu.make_async_copy(given_w, weak, lsem.at[1])
     load_b.start()
     load_w.start()
-    acc[...] = jnp.zeros_like(acc)
+    acc0[...] = jnp.zeros_like(acc0)
+    acc1[...] = jnp.zeros_like(acc1)
     rhs[...] = jnp.zeros_like(rhs)
     load_w.wait()
     load_b.wait()
@@ -402,53 +403,66 @@
         def bundle(i, carry):
             y, z = i // 4, i % 4
             b = i * 8 + xb
-            l0 = pl.multiple_of(blocks[2 * col, b] * BW, BW)
-            l1 = pl.multiple_of(blocks[2 * col + 1, b] * BW + GB * BW, BW)
+            l0 = pl.ds(pl.multiple_of(blocks[2 * col, b] * BW, BW), BW)
+            l1 = pl.ds(pl.multiple_of(blocks[2 * col + 1, b] * BW, BW), BW)
             r = pl.multiple_of(blocks[row, b] * BW, BW)
-            acc[pl.ds(r, 88), pl.ds(l0, BW)] += e0[xb, z, y]
-            acc[pl.ds(r + 88, 40), pl.ds(l0, BW)] += e1[y, xb, z, 0:40]
-            acc[pl.ds(r, 48), pl.ds(l1, BW)] += e1[y, xb, z, 40:88]
-            acc[pl.ds(r + 48, 80), pl.ds(l1, BW)] += e2[z, y, xb]
+            top, low = pl.ds(r, 88), pl.ds(r + 88, 40)
+            head, rest = pl.ds(r, 48), pl.ds(r + 48, 80)
+            v_top = acc0[top, l0] + e0[xb, z, y]
+            v_head = acc1[head, l1] + e1[y, xb, z, 40:88]
+            v_low = acc0[low, l0] + e1[y, xb, z, 0:40]
+            v_rest = acc1[rest, l1] + e2[z, y, xb]
+            acc0[top, l0] = v_top
+            acc1[head, l1] = v_head
+            acc0[low, l0] = v_low
+            acc1[rest, l1] = v_rest
             return carry
 
-        return lax.fori_loop(0, 16, bundle, carry)
+        return lax.fori_loop(0, 16, bundle, carry, unroll=4)
 
     lax.fori_loop(0, 8, batch, 0)
 
-    def copy_out(ch):
-        cols = pl.ds(pl.multiple_of(ch * 256, 256), 256)
-        return pltpu.make_async_copy(acc.at[:, cols], schur.at[:, cols], sem.at[ch])
-
-    def chunk(ch, carry):
-        cols = pl.ds(pl.multiple_of(ch * 256, 256), 256)
-        wc = w_ref[:, cols]
-        v = acc[:, cols]
-        hi = v.astype(bf16)
-        lo = (v - hi.astype(f32)).astype(bf16)
-        p_ref[...] += nt(hi, wc) + nt(lo, wc)
-
-        @pl.when(ch // 4 == row % 2)
-        def _():
-            for m in range(2):
-                k = 2 * (ch % 4) + m
-                diag[k] = acc[
-                    pl.ds(pl.multiple_of(k * BW, BW), BW),
-                    pl.ds(pl.multiple_of(ch * 256 + m * BW, BW), BW),
-                ]
-
-            @pl.when(col == row // 2)
+    def finish_half(half, acc):
+        def copy_out(ch):
+            cols = pl.ds(pl.multiple_of(ch * 256, 256), 256)
+            there = pl.ds(pl.multiple_of(half * GB * BW + ch * 256, 256), 256)
+            return pltpu.make_async_copy(
+                acc.at[:, cols], schur.at[:, there], sem.at[half * 4 + ch]
+            )
+
+        def chunk(ch, carry):
+            cols = pl.ds(pl.multiple_of(ch * 256, 256), 256)
+            wc = w_ref[:, pl.ds(pl.multiple_of(half * GB * BW + ch * 256, 256), 256)]
+            v = acc[:, cols]
+            hi = v.astype(bf16)
+            lo = (v - hi.astype(f32)).astype(bf16)
+            p_ref[...] += nt(hi, wc) + nt(lo, wc)
+
+            @pl.when(row % 2 == half)
             def _():
-                acc[:, cols] = jnp.zeros((GB * BW, 256), f32)
-
-        copy_out(ch).start()
-        return carry
-
-    lax.fori_loop(0, 8, chunk, 0)
+                for m in range(2):
+                    k = 2 * ch + m
+                    at = pl.ds(pl.multiple_of(k * BW, BW), BW)
+                    diag[k // 2, m] = acc[at, at]
+
+                @pl.when(col == row // 2)
+                def _():
+                    acc[:, cols] = jnp.zeros((GB * BW, 256), f32)
+
+            copy_out(ch).start()
+            return carry
+
+        lax.fori_loop(0, 4, chunk, 0)
+        return copy_out
+
+    outs = [finish_half(0, acc0), finish_half(1, acc1)]
     for k in range(GB):
         pt = jnp.transpose(p_ref[k * BW : (k + 1) * BW, :])
-        product[k] = pt[0:64] + pt[64:128]
-    for ch in range(8):
-        copy_out(ch).wait()
+        product[k // 2, k % 2, 0:64] = pt[0:64] + pt[64:128]
+        product[k // 2, k % 2, 64:72] = rhs[...]
+    for copy_out in outs:
+        for ch in range(4):
+            copy_out(ch).wait()
 
 
 def place(blocks, weak, e0, e1, e2, vec):
@@ -458,19 +472,20 @@
     return pl.pallas_call(
         place_kernel,
         in_specs=[hbm, hbm, vmem, vmem, vmem, vmem],
-        out_specs=(any_, vmem, vmem, vmem),
+        out_specs=(any_, vmem, vmem),
         out_shape=(
             jax.ShapeDtypeStruct((GB * BW, 2 * GB * BW), f32),
-            jax.ShapeDtypeStruct((GB, 64, BW), f32),
-            jax.ShapeDtypeStruct((GB, BW), f32),
-            jax.ShapeDtypeStruct((GB, BW, BW), f32),
+            jax.ShapeDtypeStruct((4, 2, 72, BW), f32),
+            jax.ShapeDtypeStruct((4, 2, BW, BW), f32),
         ),
         scratch_shapes=[
-            pltpu.VMEM((GB * BW, 2 * GB * BW), f32),
+            pltpu.VMEM((GB * BW, GB * BW), f32),
+            pltpu.VMEM((GB * BW, GB * BW), f32),
             pltpu.VMEM((BW, 2 * GB * BW), bf16),
             pltpu.VMEM((GB * BW, BW), f32),
             pltpu.SMEM(blocks.shape, jnp.int32),
             pltpu.VMEM(weak.shape, f32),
+            pltpu.VMEM((GB, BW), f32),
             pltpu.SemaphoreType.DMA((8,)),
             pltpu.SemaphoreType.DMA((2,)),
         ],
@@ -479,10 +494,11 @@
     )(blocks, weak, e0, e1, e2, vec)
 
 
-def finish_kernel(product, diag, part, weak, tile, rhs, got, got_r, ssem, rsem):
+def finish_kernel(product, diag, weak, tile, rhs, near, chip, far, spare, ssem, rsem):
     me = coords()
     row = lax.axis_index("row")
     mine = me["X"]
+    x, k = mine // 2, mine % 2
     owner = row // 2
     barrier, count = greet(me, ("X",))
     pl.semaphore_wait(barrier, count)
@@ -500,29 +516,28 @@
     def wait_for(ref, sem):
         pltpu.make_async_copy(ref, ref, sem).wait()
 
-    for o in WIDE:
-        to = moved(me, "X", o, 1)
-        copy(product.at[to], got.at[o - 1], 0, to).start()
-        copy(part, got_r.at[o - 1], 1, to).start()
+    copy(product.at[:, 1 - k], near, 0, moved(me, "X", 1, 1)).start()
 
     @pl.when(mine == owner)
     def _():
         for o in WIDE:
             to = moved(me, "X", o, 1)
-            copy(diag.at[to], tile, 2, to).start()
-        tile[...] = diag[mine]
-
-    wait_for(got, rsem.at[0])
-    wait_for(got_r, rsem.at[1])
-    total = product[mine]
-    total_r = part[...]
-    for o in range(7):
-        total = total + got[o]
-        total_r = total_r + got_r[o]
-    weak[...] = total
-    rhs[...] = total_r
-    wait_for(got, ssem.at[0])
-    wait_for(got_r, ssem.at[1])
+            copy(diag.at[to // 2, to % 2], tile, 2, to).start()
+        tile[...] = diag[x, k]
+
+    wait_for(near, rsem.at[0])
+    for i in range(4):
+        chip[i] = product[i, k] + near[i]
+    wait_for(near, ssem.at[0])
+    for dx in (2, 1, 3):
+        to = moved(me, "X", 2 * dx, 1)
+        copy(chip.at[to // 2], far.at[dx - 1], 1, to).start()
+    total = chip[x]
+    wait_for(far, rsem.at[1])
+    total = total + far[0] + far[1] + far[2]
+    weak[...] = total[0:64]
+    rhs[...] = total[64:72]
+    wait_for(far, ssem.at[1])
 
     @pl.when(mine != owner)
     def _():
@@ -530,10 +545,10 @@
 
     @pl.when(mine == owner)
     def _():
-        wait_for(diag.at[0:7], ssem.at[2])
-
-
-def finish(product, diag, part):
+        wait_for(spare, ssem.at[2])
+
+
+def finish(product, diag):
     vmem = pl.BlockSpec(memory_space=pltpu.VMEM)
     return pl.pallas_call(
         finish_kernel,
@@ -542,11 +557,13 @@
             jax.ShapeDtypeStruct((BW, BW), f32),
             jax.ShapeDtypeStruct((GB, BW), f32),
         ),
-        in_specs=[vmem] * 3,
+        in_specs=[vmem] * 2,
         out_specs=(vmem,) * 3,
         scratch_shapes=[
-            pltpu.VMEM((7, 64, BW), f32),
-            pltpu.VMEM((7, GB, BW), f32),
+            pltpu.VMEM((4, 72, BW), f32),
+            pltpu.VMEM((4, 72, BW), f32),
+            pltpu.VMEM((3, 72, BW), f32),
+            pltpu.VMEM((7, BW, BW), f32),
             pltpu.SemaphoreType.DMA((3,)),
             pltpu.SemaphoreType.DMA((3,)),
         ],
@@ -554,7 +571,7 @@
             collective_id=1, has_side_effects=True, vmem_limit_bytes=8 << 20
         ),
         name="finish",
-    )(product, diag, part)
+    )(product, diag)
 
 
 def emit_kernel(weak_in, tile, rhs_in, weak, layer, rhs):
@@ -587,8 +604,8 @@
 
     inputs = (glob_derivs, local_derivs, weights, residuals, track_ids)
     e = exchange(*[stay(v[0]) for v in inputs])
-    schur, product, part, diag = place(stay(module_blocks.T), stay(weak_modes.T), *e)
-    weak, layer, rhs = emit(*finish(product, diag, part))
+    schur, product, diag = place(stay(module_blocks.T), stay(weak_modes.T), *e)
+    weak, layer, rhs = emit(*finish(product, diag))
     return schur, layer, rhs.reshape(GB * BW), weak.T
 
 

time: 224 us -> 220 us (0.982)
  Pallas kernels: 222 us -> 219 us
where the time goes in v6:
time: 220 us; the launch traced here: 219 us
  Pallas kernels  219 us (100%)
    pallas_call x1, Pallas kernels, exchange(): pl.pallas_call(exchange_kernel, out_shape=tuple(shapes), in_specs=[pl.Blo...  197 us
    pallas_call x1, Pallas kernels, place(): pl.pallas_call(place_kernel, in_specs=[hbm, hbm, vmem, vmem, vmem, vmem],...  10.5 us
    pallas_call x1, Pallas kernels, finish(): pl.pallas_call(finish_kernel, out_shape=(jax.ShapeDtypeStruct((64, BW), f...  10.1 us

profile of v6, /device:TPU:17, one launch (start us, length us, event | category | flops | bytes accessed | tf_op | source)
XLA Modules:
  0.0 219.5 jit_solution(14462003836029191267)
XLA Ops:
  0.6 197.4 %exchange.1 = (f32[8,4,4,88,128]{4,3,2,1,0:T(8,128)S(1)}, f32[4,8,4,88,128]{4,3,2,1,0:T(8,128)S(1)}, f32[4,4,8,80,128]{4,3,2,1,0:T(8,128)S(1)}, f32[4,4,8,128]{3...) custom-call(bf16[16,256,128]{2,1,0:T(8,128)(2,1)} %bitcast.9, ...), custom_call_target="tpu_custom_call" | custom-call | tf_op jit(solution)/shard_map/exchange/pallas_call | solution.py:338
  198.1 10.5 %place.1 = (f32[1024,2048]{1,0:T(8,128)}, f32[4,2,72,128]{3,2,1,0:T(8,128)S(1)}, f32[4,2,128,128]{3,2,1,0:T(8,128)S(1)}) custom-call(s32[16,128]{1,0:T(8,128)} %bitcast.15, f32[64,2048]{1,0:T(8,128)} %bitcast.10, f32[8,4,4,88,128]{4,3,2,1,0:T(8,128)S(1)} %get-tuple-element.17.e0, f32[4,8,4,88,128]{4,3,2,1,0:T(8,128)S(1)} %get-tuple-element.18.e1, ...), custom_call_target="tpu_custom_call" | custom-call | tf_op jit(solution)/shard_map/place/pallas_call | solution.py:472
  208.6 10.1 %finish.1 = (f32[64,128]{1,0:T(8,128)S(1)}, f32[128,128]{1,0:T(8,128)S(1)}, f32[8,128]{1,0:T(8,128)S(1)}) custom-call(f32[4,2,72,128]{3,2,1,0:T(8,128)S(1)} %get-tuple-element.22.product, f32[4,2,128,128]{3,2,1,0:T(8,128)S(1)} %get-tuple-element.23.diag), custom_call_target="tpu_custom_call" | custom-call | tf_op jit(solution)/shard_map/finish/pallas_call | solution.py:553
  218.6 0.8 emit.1

commit v7 on v6

--- a/solution.py
+++ b/solution.py
@@ -62,19 +62,19 @@
         for i in range(LOC):
             terms.append(wa[i : i + 1, :] * a)
         terms.append(wa * r)
-        terms.append(jnp.zeros((4, PER), f32))
+        terms.append(jnp.zeros((12, PER), f32))
         stacked = jnp.concatenate(terms, axis=0)
         hot_low = jnp.where(hot, jnp.ones((), f32), zero).astype(bf16)
-        hi, mid, low = split3(stacked)
-        sums[...] += nt(hi, hot_low) + nt(mid, hot_low) + nt(low, hot_low)
+        sums[...] += nt(jnp.concatenate(split3(stacked), axis=0), hot_low)
         return carry
 
     lax.fori_loop(0, LAYERS, first, 0, unroll=UNROLL1)
 
+    total = sums[0:32] + sums[32:64] + sums[64:96]
     one = jnp.ones((1, TRK), f32)
     nil = jnp.zeros((1, TRK), f32)
     rows = [
-        [sums[4 * i + j : 4 * i + j + 1, :] + (one if i == j else nil) for j in range(LOC)]
+        [total[4 * i + j : 4 * i + j + 1, :] + (one if i == j else nil) for j in range(LOC)]
         for i in range(LOC)
     ]
     inv = [[one if i == j else nil for j in range(LOC)] for i in range(LOC)]
@@ -91,10 +91,10 @@
         inv[p] = scaled_inv
     for i in range(LOC):
         for j in range(LOC):
-            k_ref[4 * i + j : 4 * i + j + 1, :] = inv[i][j]
+            k_ref[4 * i + j : 4 * i + j + 1, :] = -inv[i][j]
     for j in range(LOC):
         q_ref[:, j * TRK : (j + 1) * TRK] = jnp.broadcast_to(
-            sums[16 + j : 17 + j, :].astype(bf16), (16, TRK)
+            total[16 + j : 17 + j, :].astype(bf16), (16, TRK)
         )
 
     def second(s, carry):
@@ -104,7 +104,7 @@
             x = h[0] * k_ref[j : j + 1, :]
             for l in range(1, LOC):
                 x = x + h[l] * k_ref[4 * l + j : 4 * l + j + 1, :]
-            x_all[row, j * TRK : (j + 1) * TRK] = (-x).astype(bf16)
+            x_all[row, j * TRK : (j + 1) * TRK] = x.astype(bf16)
         return carry
 
     lax.fori_loop(0, LAYERS, second, 0, unroll=UNROLL2)
@@ -347,7 +347,7 @@
             pltpu.VMEM((LAYERS * BW, LOC * TRK), bf16),
             pltpu.VMEM((4, 4, 8, BW), f32),
             pltpu.VMEM((4, 4, 8, BW), f32),
-            pltpu.VMEM((24, TRK), f32),
+            pltpu.VMEM((96, TRK), f32),
             pltpu.VMEM((16, LOC * TRK), bf16),
             pltpu.VMEM((16, TRK), f32),
             pltpu.SemaphoreType.DMA((3, 3)),
@@ -384,13 +384,7 @@
     acc0[...] = jnp.zeros_like(acc0)
     acc1[...] = jnp.zeros_like(acc1)
     rhs[...] = jnp.zeros_like(rhs)
-    load_w.wait()
     load_b.wait()
-    w = weak[...]
-    w_hi = w.astype(bf16)
-    w_ref[0:64, :] = w_hi
-    w_ref[64:128, :] = (w - w_hi.astype(f32)).astype(bf16)
-    p_ref[...] = jnp.zeros_like(p_ref)
 
     def term(i, carry):
         k = blocks[row, i * 8 + col]
@@ -421,6 +415,13 @@
         return lax.fori_loop(0, 16, bundle, carry, unroll=4)
 
     lax.fori_loop(0, 8, batch, 0)
+    load_w.wait()
+    w = weak[...]
+    w_hi = w.astype(bf16)
+    w_ref[0:64, :] = w_hi
+    w_ref[64:128, :] = (w - w_hi.astype(f32)).astype(bf16)
+    p_ref[...] = jnp.zeros_like(p_ref)
+
 
     def finish_half(half, acc):
         def copy_out(ch):

time: 220 us -> 219 us (level)
  no operation moved by 1% of the time
where the time goes in v7:
time: 219 us; the launch traced here: 218 us
  Pallas kernels  217 us (99%)
    pallas_call x1, Pallas kernels, exchange(): pl.pallas_call(exchange_kernel, out_shape=tuple(shapes), in_specs=[pl.Blo...  196 us
    pallas_call x1, Pallas kernels, place(): pl.pallas_call(place_kernel, in_specs=[hbm, hbm, vmem, vmem, vmem, vmem],...  10.2 us
    pallas_call x1, Pallas kernels, finish(): pl.pallas_call(finish_kernel, out_shape=(jax.ShapeDtypeStruct((64, BW), f...  10.1 us

profile of v7, /device:TPU:17, one launch (start us, length us, event | category | flops | bytes accessed | tf_op | source)
XLA Modules:
  0.0 218.1 jit_solution(11030906482374556567)
XLA Ops:
  0.6 196.3 %exchange.1 = (f32[8,4,4,88,128]{4,3,2,1,0:T(8,128)S(1)}, f32[4,8,4,88,128]{4,3,2,1,0:T(8,128)S(1)}, f32[4,4,8,80,128]{4,3,2,1,0:T(8,128)S(1)}, f32[4,4,8,128]{3...) custom-call(bf16[16,256,128]{2,1,0:T(8,128)(2,1)} %bitcast.9, ...), custom_call_target="tpu_custom_call" | custom-call | tf_op jit(solution)/shard_map/exchange/pallas_call | solution.py:338
  196.9 10.2 %place.1 = (f32[1024,2048]{1,0:T(8,128)}, f32[4,2,72,128]{3,2,1,0:T(8,128)S(1)}, f32[4,2,128,128]{3,2,1,0:T(8,128)S(1)}) custom-call(s32[16,128]{1,0:T(8,128)} %bitcast.15, f32[64,2048]{1,0:T(8,128)} %bitcast.10, f32[8,4,4,88,128]{4,3,2,1,0:T(8,128)S(1)} %get-tuple-element.17.e0, f32[4,8,4,88,128]{4,3,2,1,0:T(8,128)S(1)} %get-tuple-element.18.e1, ...), custom_call_target="tpu_custom_call" | custom-call | tf_op jit(solution)/shard_map/place/pallas_call | solution.py:473
  207.1 10.1 %finish.1 = (f32[64,128]{1,0:T(8,128)S(1)}, f32[128,128]{1,0:T(8,128)S(1)}, f32[8,128]{1,0:T(8,128)S(1)}) custom-call(f32[4,2,72,128]{3,2,1,0:T(8,128)S(1)} %get-tuple-element.22.product, f32[4,2,128,128]{3,2,1,0:T(8,128)S(1)} %get-tuple-element.23.diag), custom_call_target="tpu_custom_call" | custom-call | tf_op jit(solution)/shard_map/finish/pallas_call | solution.py:554
  217.3 0.8 emit.1

commit v8 on v7

--- a/solution.py
+++ b/solution.py
@@ -386,13 +386,6 @@
     rhs[...] = jnp.zeros_like(rhs)
     load_b.wait()
 
-    def term(i, carry):
-        k = blocks[row, i * 8 + col]
-        rhs[pl.ds(k, 1), :] += vec[i % 4, i // 4, 0:1]
-        return carry
-
-    lax.fori_loop(0, 16, term, 0)
-
     def batch(xb, carry):
         def bundle(i, carry):
             y, z = i // 4, i % 4
@@ -431,6 +424,13 @@
                 acc.at[:, cols], schur.at[:, there], sem.at[half * 4 + ch]
             )
 
+        owner = (row % 2 == half) & (col == row // 2)
+
+        @pl.when(jnp.logical_not(owner))
+        def _():
+            for ch in range(4):
+                copy_out(ch).start()
+
         def chunk(ch, carry):
             cols = pl.ds(pl.multiple_of(ch * 256, 256), 256)
             wc = w_ref[:, pl.ds(pl.multiple_of(half * GB * BW + ch * 256, 256), 256)]
@@ -446,17 +446,24 @@
                     at = pl.ds(pl.multiple_of(k * BW, BW), BW)
                     diag[k // 2, m] = acc[at, at]
 
-                @pl.when(col == row // 2)
-                def _():
-                    acc[:, cols] = jnp.zeros((GB * BW, 256), f32)
-
-            copy_out(ch).start()
+            @pl.when(owner)
+            def _():
+                acc[:, cols] = jnp.zeros((GB * BW, 256), f32)
+                copy_out(ch).start()
+
             return carry
 
         lax.fori_loop(0, 4, chunk, 0)
         return copy_out
 
     outs = [finish_half(0, acc0), finish_half(1, acc1)]
+
+    def term(i, carry):
+        k = blocks[row, i * 8 + col]
+        rhs[pl.ds(k, 1), :] += vec[i % 4, i // 4, 0:1]
+        return carry
+
+    lax.fori_loop(0, 16, term, 0)
     for k in range(GB):
         pt = jnp.transpose(p_ref[k * BW : (k + 1) * BW, :])
         product[k // 2, k % 2, 0:64] = pt[0:64] + pt[64:128]

time: 219 us -> 218 us (level)
  no operation moved by 1% of the time
where the time goes in v8:
time: 218 us; the launch traced here: 217 us
  Pallas kernels  217 us (100%)
    pallas_call x1, Pallas kernels, exchange(): pl.pallas_call(exchange_kernel, out_shape=tuple(shapes), in_specs=[pl.Blo...  196 us
    pallas_call x1, Pallas kernels, finish(): pl.pallas_call(finish_kernel, out_shape=(jax.ShapeDtypeStruct((64, BW), f...  10.1 us
    pallas_call x1, Pallas kernels, place(): pl.pallas_call(place_kernel, in_specs=[hbm, hbm, vmem, vmem, vmem, vmem],...  9.46 us

profile of v8, /device:TPU:17, one launch (start us, length us, event | category | flops | bytes accessed | tf_op | source)
XLA Modules:
  0.0 217.3 jit_solution(13119544469959569451)
XLA Ops:
  0.6 196.3 %exchange.1 = (f32[8,4,4,88,128]{4,3,2,1,0:T(8,128)S(1)}, f32[4,8,4,88,128]{4,3,2,1,0:T(8,128)S(1)}, f32[4,4,8,80,128]{4,3,2,1,0:T(8,128)S(1)}, f32[4,4,8,128]{3...) custom-call(bf16[16,256,128]{2,1,0:T(8,128)(2,1)} %bitcast.9, ...), custom_call_target="tpu_custom_call" | custom-call | tf_op jit(solution)/shard_map/exchange/pallas_call | solution.py:338
  196.9 9.5 %place.1 = (f32[1024,2048]{1,0:T(8,128)}, f32[4,2,72,128]{3,2,1,0:T(8,128)S(1)}, f32[4,2,128,128]{3,2,1,0:T(8,128)S(1)}) custom-call(s32[16,128]{1,0:T(8,128)} %bitcast.15, f32[64,2048]{1,0:T(8,128)} %bitcast.10, f32[8,4,4,88,128]{4,3,2,1,0:T(8,128)S(1)} %get-tuple-element.17.e0, f32[4,8,4,88,128]{4,3,2,1,0:T(8,128)S(1)} %get-tuple-element.18.e1, ...), custom_call_target="tpu_custom_call" | custom-call | tf_op jit(solution)/shard_map/place/pallas_call | solution.py:480
  206.4 10.1 %finish.1 = (f32[64,128]{1,0:T(8,128)S(1)}, f32[128,128]{1,0:T(8,128)S(1)}, f32[8,128]{1,0:T(8,128)S(1)}) custom-call(f32[4,2,72,128]{3,2,1,0:T(8,128)S(1)} %get-tuple-element.22.product, f32[4,2,128,128]{3,2,1,0:T(8,128)S(1)} %get-tuple-element.23.diag), custom_call_target="tpu_custom_call" | custom-call | tf_op jit(solution)/shard_map/finish/pallas_call | solution.py:561
  216.5 0.8 emit.1
